TPU v7x, 512 devices: a whole 4x8x8 slice. The times are simulated.
512 devices in a mesh: layer: 2 (over core), row: 16 (over x, z_hi), col: 16 (over z_lo, y).
Axes of the slice: x: 4, y: 8, z: 8 (z_hi: 4, z_lo: 2; z = z_hi * 2 + z_lo), core: 2. Of those that a mesh axis runs over, the one named last changes fastest.
Arguments:
- rhs_sub: float32 [2, 3, 1, 16, 256, 512], P('layer', None, None, 'row', 'col'), may hold values from -6 to 6
- rhs_top: float32 [1, 16, 256, 512], P(None, 'row', 'col'), may hold values from -6 to 6
- lower_inv_sub: float32 [2, 3, 1, 16, 256, 256], P('layer', None, None, 'row', 'col'), as said below
- lower_inv_top: float32 [1, 16, 256, 256], P(None, 'row', 'col'), as said below
- upper_inv_sub: float32 [2, 3, 1, 16, 256, 256], P('layer', None, None, 'row', 'col'), as said below
- upper_inv_top: float32 [1, 16, 256, 256], P(None, 'row', 'col'), as said below
- lower_sub: float32 [2, 3, 1, 16, 1, 16, 256, 256], P('layer', None, None, 'row', None, 'col'), may hold values from -0.09375 to 0.09375
- lower_top: float32 [2, 3, 1, 16, 1, 16, 256, 256], P('layer', None, None, 'row', None, 'col'), may hold values from -0.0546875 to 0.0546875
- upper_sub: float32 [2, 3, 1, 16, 1, 16, 256, 256], P('layer', None, None, 'row', None, 'col'), may hold values from -0.0625 to 0.0625
- upper_top: float32 [2, 3, 1, 16, 1, 16, 256, 256], P('layer', None, None, 'row', None, 'col'), may hold values from -0.09375 to 0.09375
- block_pattern: int32 [2, 4, 3, 1, 16, 1, 16], P('layer', None, None, None, 'row', None, 'col'), may hold values 0 or 1
Outputs:
- solution_sub: float32 [2, 3, 1, 16, 256, 512], P('layer', None, None, 'row', 'col')
- solution_top: float32 [1, 16, 256, 512], P(None, 'row', 'col')
Inputs may be any that keep to these rules, and one draw needn't show every extreme that they name: `lower_inv_sub`: every 256 x 256 block is lower triangular with unit diagonal. `lower_inv_top`: every 256 x 256 block is lower triangular with unit diagonal. `upper_inv_sub`: every 256 x 256 block is upper triangular with unit diagonal. `upper_inv_top`: every 256 x 256 block is upper triangular with unit diagonal.
All inputs are finite; a program needn't handle non-finite values. No bound on the sum of `block_pattern` on one device may be relied on, other than what follows from the above.
Results may differ from a plain program's by a relative error of at most 0.00014.
Values sent between devices are 32-bit elements; how exact they have to be, the bound alone decides.
No kernel may reach another device: no remote copies, remote signals or barrier semaphores. Data moves between devices by JAX's collectives and lax.ppermute only.
A program may use at most 64 MiB of HBM per device.

v0:
```python
import jax
import jax.numpy as jnp
from jax import lax
from jax.sharding import PartitionSpec as P

HIGHEST = lax.Precision.HIGHEST


def broadcast(x, axis, root):
    mine = lax.axis_index(axis) == root
    return lax.psum(jnp.where(mine, x, jnp.zeros_like(x)), axis)


def couple(blocks, pattern, solution):
    weighted = solution[None] * pattern[:, :, None, None].astype(jnp.float32)
    return jnp.einsum("tsab,tsbn->tan", blocks, weighted, precision=HIGHEST)


def spread(whole_block):
    return broadcast(whole_block, "row", lax.axis_index("col"))


def on_device(
    rhs_sub,
    rhs_top,
    lower_inv_sub,
    lower_inv_top,
    upper_inv_sub,
    upper_inv_top,
    lower_sub,
    lower_top,
    upper_sub,
    upper_top,
    block_pattern,
):
    lower_list = [lower_inv_sub[0, level, :, 0] for level in range(3)] + [lower_inv_top[:, 0]]
    upper_list = [upper_inv_sub[0, level, :, 0] for level in range(3)] + [upper_inv_top[:, 0]]
    right_sides = [rhs_sub[0, level, :, 0] for level in range(3)] + [rhs_top[:, 0]]

    def solve(partial_value, right_side, inverse_rows, top):
        if partial_value is None:
            residual = right_side
        else:
            share = lax.psum_scatter(partial_value, "col", scatter_dimension=1, tiled=True)
            if top:
                share = lax.psum(share, "layer")
            residual = right_side - share
        return jnp.einsum(
            "kab,kbn->kan",
            inverse_rows,
            lax.all_gather(residual, "col", axis=1, tiled=True),
            precision=HIGHEST,
        )

    def copy_out(solution):
        return spread(lax.all_gather(solution, "col", axis=1, tiled=True))

    def blocks(array, pair):
        return array[0, pair, :, 0, :, 0]

    def pattern(kind, pair):
        return block_pattern[0, kind, pair, :, 0, :, 0]

    fore_zero = solve(None, right_sides[0], lower_list[0], False)
    copy_zero = copy_out(fore_zero)
    into_one = couple(blocks(lower_sub, 0), pattern(0, 0), copy_zero)
    into_two = couple(blocks(lower_sub, 1), pattern(0, 1), copy_zero)
    into_top = couple(blocks(lower_top, 0), pattern(1, 0), copy_zero)
    fore_one = solve(into_one, right_sides[1], lower_list[1], False)
    copy_one = copy_out(fore_one)
    into_two = into_two + couple(blocks(lower_sub, 2), pattern(0, 2), copy_one)
    into_top = into_top + couple(blocks(lower_top, 1), pattern(1, 1), copy_one)
    fore_two = solve(into_two, right_sides[2], lower_list[2], False)
    copy_two = copy_out(fore_two)
    into_top = into_top + couple(blocks(lower_top, 2), pattern(1, 2), copy_two)
    fore_top = solve(into_top, right_sides[3], lower_list[3], True)
    final_top = solve(None, fore_top, upper_list[3], False)
    down_top = copy_out(final_top)
    toward_two = couple(blocks(upper_top, 2), pattern(3, 2), down_top)
    toward_one = couple(blocks(upper_top, 1), pattern(3, 1), down_top)
    toward_zero = couple(blocks(upper_top, 0), pattern(3, 0), down_top)
    final_two = solve(toward_two, fore_two, upper_list[2], False)
    down_two = copy_out(final_two)
    toward_one = toward_one + couple(blocks(upper_sub, 2), pattern(2, 2), down_two)
    toward_zero = toward_zero + couple(blocks(upper_sub, 1), pattern(2, 1), down_two)
    final_one = solve(toward_one, fore_one, upper_list[1], False)
    down_one = copy_out(final_one)
    toward_zero = toward_zero + couple(blocks(upper_sub, 0), pattern(2, 0), down_one)
    final_zero = solve(toward_zero, fore_zero, upper_list[0], False)
    solution_sub = jnp.stack([final_zero, final_one, final_two])[None, :, :, None]
    solution_top = final_top[:, None]
    return (solution_sub, solution_top)


def solution(mesh):
    placed = (
        P("layer", None, None, "row", "col", None),
        P(None, "row", "col", None),
        P("layer", None, None, "row", "col", None),
        P(None, "row", "col", None),
        P("layer", None, None, "row", "col", None),
        P(None, "row", "col", None),
        P("layer", None, None, "row", None, "col", None, None),
        P("layer", None, None, "row", None, "col", None, None),
        P("layer", None, None, "row", None, "col", None, None),
        P("layer", None, None, "row", None, "col", None, None),
        P("layer", None, None, None, "row", None, "col"),
    )
    return jax.shard_map(
        on_device,
        mesh=mesh,
        in_specs=placed,
        out_specs=(P("layer", None, None, "row", "col", None), P(None, "row", "col", None)),
        check_vma=False,
    )
```

profile of v0, /device:TPU:6, one launch (start us, length us, event | category | flops | bytes accessed | tf_op | source)
XLA Modules:
  0.0 2183.9 jit_solution(2908091870607377560)
XLA Ops:
  7.2 0.8 fusion.100
  8.0 37.7 %all-gather = f32[1,1,1,1,256,512]{5,4,3,2,1,0:T(8,128)S(1)} all-gather(f32[1,1,1,1,16,512]{5,4,3,2,1,0:T(8,128)S(1)} %get-tuple-element.8), channel_id=2, replica_groups=mesh['layer'=2,'row'=16,'col'=16] {'col'}, dimensions={4}, use_global_device_ids=true | all-gather | bytes 557056 | tf_op jit(solution)/shard_map/all_gather | solution.py:51
  46.1 32.3 %all-gather.1 = f32[256,512]{1,0:T(8,128)S(1)} all-gather(f32[16,512]{1,0:T(8,128)S(1)} %fusion.33), channel_id=3, replica_groups=mesh['layer'=2,'row'=16,'col'=16] {'col'}, dimensions={0}, use_global_device_ids=true | all-gather | bytes 557056 | tf_op jit(solution)/shard_map/all_gather | solution.py:56
  78.4 0.8 select_bitcast_fusion.5
  79.3 0.6 copy-done.13
  79.9 0.7 fusion.101
  81.3 168.5 %all-reduce.13.cloned.1.call-done = f32[1,256,512]{2,1,0:T(8,128)} async-done(((f32[1,256,512]{2,1,0:T(8,128)}), f32[1,256,512]{2,1,0:T(8,128)}) %all-reduce.13.cloned.1.call-update) | async-done | bytes 524304 | tf_op jit(solution)/shard_map/psum | solution.py:11
  249.8 2.0 convolution_bitcast_fusion.1
  251.8 1.0 copy.24
  253.0 1.3 dynamic-slice
  254.9 140.9 %all-reduce.25.cloned.1.call-done = f32[1,256,512]{2,0,1:T(1,128)} async-done(((f32[1,256,512]{2,0,1:T(1,128)}), f32[1,256,512]{2,0,1:T(1,128)}) %all-reduce.25.cloned.1.call-update) | async-done | bytes 524304
  395.9 0.8 fusion.84
  396.7 35.3 %all_gather.44 = f32[1,256,512]{2,0,1:T(1,128)S(1)} all-gather(f32[1,16,512]{2,0,1:T(1,128)S(1)} %fusion.84), channel_id=1, replica_groups=mesh['layer'=2,'row'=16,'col'=16] {'col'}, dimensions={1}, use_global_device_ids=true | all-gather | bytes 557056 | tf_op jit(solution)/shard_map/all_gather | solution.py:51
  432.0 0.4 fusion.9
  432.4 32.3 %all-gather.2 = f32[256,512]{1,0:T(8,128)S(1)} all-gather(f32[16,512]{1,0:T(8,128)S(1)} %bitcast.205), channel_id=4, replica_groups=mesh['layer'=2,'row'=16,'col'=16] {'col'}, dimensions={0}, use_global_device_ids=true | all-gather | bytes 557056 | tf_op jit(solution)/shard_map/all_gather | solution.py:56
  464.7 0.9 select_bitcast_fusion.4
  466.9 1.0 fusion.27
  468.0 165.0 %all-reduce.15.cloned.1.call-done = f32[1,256,512]{2,1,0:T(8,128)} async-done(((f32[1,256,512]{2,1,0:T(8,128)}), f32[1,256,512]{2,1,0:T(8,128)}) %all-reduce.15.cloned.1.call-update) | async-done | bytes 524304 | tf_op jit(solution)/shard_map/psum | solution.py:11
  633.0 2.0 fusion.3
  635.0 1.0 copy.26
  638.0 141.0 %all-reduce.27.cloned.1.call-done = f32[1,256,512]{2,0,1:T(1,128)} async-done(((f32[1,256,512]{2,0,1:T(1,128)}), f32[1,256,512]{2,0,1:T(1,128)}) %all-reduce.27.cloned.1.call-update) | async-done | bytes 524304
  779.1 0.8 fusion.83
  779.9 35.3 %all_gather.46 = f32[1,256,512]{2,0,1:T(1,128)S(1)} all-gather(f32[1,16,512]{2,0,1:T(1,128)S(1)} %fusion.83), channel_id=1, replica_groups=mesh['layer'=2,'row'=16,'col'=16] {'col'}, dimensions={1}, use_global_device_ids=true | all-gather | bytes 557056 | tf_op jit(solution)/shard_map/all_gather | solution.py:51
  815.2 0.4 fusion.6
  815.6 32.3 %all-gather.3 = f32[256,512]{1,0:T(8,128)S(1)} all-gather(f32[16,512]{1,0:T(8,128)S(1)} %bitcast.206), channel_id=5, replica_groups=mesh['layer'=2,'row'=16,'col'=16] {'col'}, dimensions={0}, use_global_device_ids=true | all-gather | bytes 557056 | tf_op jit(solution)/shard_map/all_gather | solution.py:56
  847.9 0.9 select_bitcast_fusion.3
  849.2 1.0 fusion.31
  850.3 1.0 convolution_add_fusion.5
  851.3 164.9 %all-reduce.17.cloned.1.call-done = f32[1,256,512]{2,1,0:T(8,128)} async-done(((f32[1,256,512]{2,1,0:T(8,128)}), f32[1,256,512]{2,1,0:T(8,128)}) %all-reduce.17.cloned.1.call-update) | async-done | bytes 524304 | tf_op jit(solution)/shard_map/psum | solution.py:11
  1016.2 2.0 fusion.2
  1018.2 1.1 copy.27
  1019.4 142.9 %all-reduce.29.cloned.1.call-done = f32[1,256,512]{2,0,1:T(1,128)} async-done(((f32[1,256,512]{2,0,1:T(1,128)}), f32[1,256,512]{2,0,1:T(1,128)}) %all-reduce.29.cloned.1.call-update) | async-done | bytes 524304
  1162.3 0.8 constant_dynamic-slice_fusion
  1163.0 3.5 psum.52
  1166.6 35.3 %all_gather.48 = f32[1,256,512]{2,0,1:T(1,128)S(1)} all-gather(f32[1,16,512]{2,0,1:T(1,128)S(1)} %reshape_subtract_fusion), channel_id=1, replica_groups=mesh['layer'=2,'row'=16,'col'=16] {'col'}, dimensions={1}, use_global_device_ids=true | all-gather | bytes 557056 | tf_op jit(solution)/shard_map/all_gather | solution.py:51
  1201.9 0.4 convolution_bitcast_fusion.3
  1202.3 32.8 %all-gather.4 = f32[256,512]{1,0:T(8,128)S(1)} all-gather(f32[16,512]{1,0:T(8,128)S(1)} %convolution_bitcast_fusion.3), channel_id=6, replica_groups=mesh['layer'=2,'row'=16,'col'=16] {'col'}, dimensions={0}, use_global_device_ids=true | all-gather | bytes 557056 | tf_op jit(solution)/shard_map/all_gather | solution.py:51
  1235.0 0.4 fusion.88
  1235.4 34.6 %all-gather.5 = f32[256,512]{1,0:T(8,128)S(1)} all-gather(f32[16,512]{1,0:T(8,128)S(1)} %bitcast.211), channel_id=7, replica_groups=mesh['layer'=2,'row'=16,'col'=16] {'col'}, dimensions={0}, use_global_device_ids=true | all-gather | bytes 557056 | tf_op jit(solution)/shard_map/all_gather | solution.py:56
  1270.0 0.8 select_bitcast_fusion.2
  1271.5 165.3 %all-reduce.19.cloned.1.call-done = f32[1,256,512]{2,1,0:T(8,128)} async-done(((f32[1,256,512]{2,1,0:T(8,128)}), f32[1,256,512]{2,1,0:T(8,128)}) %all-reduce.19.cloned.1.call-update) | async-done | bytes 524304 | tf_op jit(solution)/shard_map/psum | solution.py:11
  1436.8 2.5 convolution_bitcast_fusion
  1439.4 75.2 %reduce-scatter.4.cloned.1.call-done = f32[1,16,512]{2,1,0:T(8,128)} async-done(((f32[1,256,512]{2,1,0:T(8,128)}), f32[1,16,512]{2,1,0:T(8,128)}) %reduce-scatter.4.cloned.1.call-update) | async-done | bytes 32784 | tf_op jit(solution)/shard_map/reduce_scatter | solution.py:44
  1514.6 0.8 bitcast_subtract_fusion.1
  1515.3 34.0 %all_gather.51 = f32[1,256,512]{2,1,0:T(8,128)S(1)} all-gather(f32[1,16,512]{2,1,0:T(8,128)S(1)} %bitcast_subtract_fusion.1), channel_id=1, replica_groups=mesh['layer'=2,'row'=16,'col'=16] {'col'}, dimensions={1}, use_global_device_ids=true | all-gather | bytes 557056 | tf_op jit(solution)/shard_map/all_gather | solution.py:51
  1549.3 0.4 fusion.20
  1549.7 33.2 %all-gather.6 = f32[256,512]{1,0:T(8,128)S(1)} all-gather(f32[16,512]{1,0:T(8,128)S(1)} %bitcast.207), channel_id=8, replica_groups=mesh['layer'=2,'row'=16,'col'=16] {'col'}, dimensions={0}, use_global_device_ids=true | all-gather | bytes 557056 | tf_op jit(solution)/shard_map/all_gather | solution.py:56
  1582.9 0.9 select_bitcast_fusion.1
  1585.6 0.7 fusion.17
  1586.2 164.1 %all-reduce.21.cloned.1.call-done = f32[1,256,512]{2,1,0:T(8,128)} async-done(((f32[1,256,512]{2,1,0:T(8,128)}), f32[1,256,512]{2,1,0:T(8,128)}) %all-reduce.21.cloned.1.call-update) | async-done | bytes 524304 | tf_op jit(solution)/shard_map/psum | solution.py:11
  1750.3 2.5 fusion.1
  1754.7 73.2 %reduce-scatter.6.cloned.1.call-done = f32[1,16,512]{2,1,0:T(8,128)} async-done(((f32[1,256,512]{2,1,0:T(8,128)}), f32[1,16,512]{2,1,0:T(8,128)}) %reduce-scatter.6.cloned.1.call-update) | async-done | bytes 32784 | tf_op jit(solution)/shard_map/reduce_scatter | solution.py:44
  1827.8 0.8 bitcast_subtract_fusion
  1828.6 34.1 %all_gather.53 = f32[1,256,512]{2,1,0:T(8,128)S(1)} all-gather(f32[1,16,512]{2,1,0:T(8,128)S(1)} %bitcast_subtract_fusion), channel_id=1, replica_groups=mesh['layer'=2,'row'=16,'col'=16] {'col'}, dimensions={1}, use_global_device_ids=true | all-gather | bytes 557056 | tf_op jit(solution)/shard_map/all_gather | solution.py:51
  1863.0 33.2 %all-gather.7 = f32[256,512]{1,0:T(8,128)S(1)} all-gather(f32[16,512]{1,0:T(8,128)S(1)} %bitcast.209), channel_id=9, replica_groups=mesh['layer'=2,'row'=16,'col'=16] {'col'}, dimensions={0}, use_global_device_ids=true | all-gather | bytes 557056 | tf_op jit(solution)/shard_map/all_gather | solution.py:56
  1896.2 0.9 select_bitcast_fusion
  1897.2 0.7 fusion.23
  1898.2 0.7 convolution_add_fusion.2
  1898.9 165.1 %all-reduce.23.cloned.1.call-done = f32[1,256,512]{2,1,0:T(8,128)} async-done(((f32[1,256,512]{2,1,0:T(8,128)}), f32[1,256,512]{2,1,0:T(8,128)}) %all-reduce.23.cloned.1.call-update) | async-done | bytes 524304 | tf_op jit(solution)/shard_map/psum | solution.py:11
  2064.0 2.5 fusion
  2066.5 75.0 %reduce-scatter.8.cloned.1.call-done = f32[1,16,512]{2,1,0:T(8,128)} async-done(((f32[1,256,512]{2,1,0:T(8,128)}), f32[1,16,512]{2,1,0:T(8,128)}) %reduce-scatter.8.cloned.1.call-update) | async-done | bytes 32784 | tf_op jit(solution)/shard_map/reduce_scatter | solution.py:44
  2141.6 0.8 bitcast_subtract_fusion.2
  2142.3 33.7 %all_gather.55 = f32[1,256,512]{2,1,0:T(8,128)S(1)} all-gather(f32[1,16,512]{2,1,0:T(8,128)S(1)} %bitcast_subtract_fusion.2), channel_id=1, replica_groups=mesh['layer'=2,'row'=16,'col'=16] {'col'}, dimensions={1}, use_global_device_ids=true | all-gather | bytes 557056 | tf_op jit(solution)/shard_map/all_gather | solution.py:51
  2176.4 0.7 maximum_bitcast_fusion
  (57 shorter events, 2.9 us)
Async XLA Ops:
  7.2 1194.7 %copy-start = (f32[1,1,16,256]{3,2,1,0:T(8,128)S(1)}, f32[1,1,16,256]{3,2,1,0:T(8,128)}, u32[]{:S(2)}) copy-start(f32[1,1,16,256]{3,2,1,0:T(8,128)} %param.14) | copy-start | bytes 49156
  7.2 242.6 %all-reduce.13.cloned.1.call-start = ((), (), s32[]{:S(2)}) async-start(), calls=%async_computation.3 | async-start | bytes 1048576 | tf_op jit(solution)/shard_map/psum | solution.py:11
  8.0 37.7 %copy-start.10 = (f32[1,3,1,1,16,256]{5,4,3,2,1,0:T(8,128)S(1)}, f32[1,3,1,1,16,256]{5,4,3,2,1,0:T(8,128)}, u32[]{:S(2)}) copy-start(f32[1,3,1,1,16,256]{5,4,3,2,1,0:T(8,128)} %param.13) | copy-start | bytes 147460
  78.4 171.4 %copy-start.6 = (f32[1,3,1,1,1,1,256,256]{7,6,5,4,3,2,1,0:T(8,128)S(1)}, f32[1,3,1,1,1,1,256,256]{7,6,5,4,3,2,1,0:T(8,128)}, u32[]{:S(2)}) copy-start(f32[1,3,1,1,1,1,256,256]{7,6,5,4,3,2,1,0:T(8,128)} %param.17) | copy-start | bytes 2359300
  79.3 0.7 copy-start.13
  79.3 316.6 %all-reduce.25.cloned.1.call-start = ((), (), s32[]{:S(2)}) async-start(), calls=%async_computation.12 | async-start | bytes 1048576
  252.9 380.1 %all-reduce.15.cloned.1.call-start = ((), (), s32[]{:S(2)}) async-start(), calls=%async_computation.4 | async-start | bytes 1048576 | tf_op jit(solution)/shard_map/psum | solution.py:11
  465.6 1.4 copy-start.1
  465.6 313.5 %all-reduce.27.cloned.1.call-start = ((), (), s32[]{:S(2)}) async-start(), calls=%async_computation.13 | async-start | bytes 1048576
  636.1 380.1 %all-reduce.17.cloned.1.call-start = ((), (), s32[]{:S(2)}) async-start(), calls=%async_computation.5 | async-start | bytes 1048576 | tf_op jit(solution)/shard_map/psum | solution.py:11
  847.9 1.3 copy-start.7
  848.8 313.5 %all-reduce.29.cloned.1.call-start = ((), (), s32[]{:S(2)}) async-start(), calls=%async_computation.14 | async-start | bytes 1048576
  849.2 1.0 copy-start.3
  1019.3 417.5 %all-reduce.19.cloned.1.call-start = ((), (), s32[]{:S(2)}) async-start(), calls=%async_computation.6 | async-start | bytes 1048576 | tf_op jit(solution)/shard_map/psum | solution.py:11
  1163.0 3.5 copy-start.12
  1202.3 32.8 %copy-start.14 = (f32[1,1,16,256]{3,2,1,0:T(8,128)S(1)}, f32[1,1,16,256]{3,2,1,0:T(8,128)}, u32[]{:S(2)}) copy-start(f32[1,1,16,256]{3,2,1,0:T(8,128)} %param.16) | copy-start | bytes 49156
  1235.4 34.6 %copy-start.9 = (f32[512,16]{0,1:T(8,128)}, f32[512,16]{0,1:T(8,128)S(1)}, u32[]{:S(2)}) copy-start(f32[512,16]{0,1:T(8,128)S(1)} %fusion.88) | copy-start | bytes 98308
  1270.0 166.8 %copy-start.5 = (f32[1,3,1,1,1,1,256,256]{7,6,5,4,3,2,1,0:T(8,128)S(1)}, f32[1,3,1,1,1,1,256,256]{7,6,5,4,3,2,1,0:T(8,128)}, u32[]{:S(2)}) copy-start(f32[1,3,1,1,1,1,256,256]{7,6,5,4,3,2,1,0:T(8,128)} %param.20) | copy-start | bytes 2359300
  1270.9 243.7 %reduce-scatter.4.cloned.1.call-start = ((), (), s32[]{:S(2)}) async-start(), calls=%async_computation.7 | async-start | bytes 557056 | tf_op jit(solution)/shard_map/reduce_scatter | solution.py:44
  1439.4 310.9 %all-reduce.21.cloned.1.call-start = ((), (), s32[]{:S(2)}) async-start(), calls=%async_computation.8 | async-start | bytes 1048576 | tf_op jit(solution)/shard_map/psum | solution.py:11
  1515.3 34.0 %copy-start.11 = (f32[1,3,1,1,16,256]{5,4,3,2,1,0:T(8,128)S(1)}, f32[1,3,1,1,16,256]{5,4,3,2,1,0:T(8,128)}, u32[]{:S(2)}) copy-start(f32[1,3,1,1,16,256]{5,4,3,2,1,0:T(8,128)} %param.15) | copy-start | bytes 147460
  1583.8 1.8 copy-start.2
  1583.8 166.5 %copy-start.8 = (f32[1,3,1,1,1,1,256,256]{7,6,5,4,3,2,1,0:T(8,128)S(1)}, f32[1,3,1,1,1,1,256,256]{7,6,5,4,3,2,1,0:T(8,128)}, u32[]{:S(2)}) copy-start(f32[1,3,1,1,1,1,256,256]{7,6,5,4,3,2,1,0:T(8,128)} %param.19) | copy-start | bytes 2359300
  1583.8 244.0 %reduce-scatter.6.cloned.1.call-start = ((), (), s32[]{:S(2)}) async-start(), calls=%async_computation.9 | async-start | bytes 557056 | tf_op jit(solution)/shard_map/reduce_scatter | solution.py:44
  1752.8 311.2 %all-reduce.23.cloned.1.call-start = ((), (), s32[]{:S(2)}) async-start(), calls=%async_computation.10 | async-start | bytes 1048576 | tf_op jit(solution)/shard_map/psum | solution.py:11
  1897.1 244.5 %reduce-scatter.8.cloned.1.call-start = ((), (), s32[]{:S(2)}) async-start(), calls=%async_computation.11 | async-start | bytes 557056 | tf_op jit(solution)/shard_map/reduce_scatter | solution.py:44
  1897.2 1.0 copy-start.4
Sparse Core Ops, SparseCore 0:
  79.4 170.3 all-reduce.12
  253.0 142.7 all-reduce.24
  465.7 167.2 all-reduce.14
  636.2 142.7 all-reduce.26
  848.9 167.2 all-reduce.16
  1019.4 142.7 all-reduce.28
  1271.0 165.8 all-reduce.18
  1439.6 74.8 reduce-scatter.3
  1583.9 166.3 all-reduce.20
  1752.9 74.8 reduce-scatter.5
  1897.2 166.7 all-reduce.22
  2066.7 74.8 reduce-scatter.7
where the time goes:
time: 2190 us; the launch traced here: 2180 us
  waiting for transfers between devices  1640 us (75%)
  blocking collectives  480 us (22%)
  between operations  22.8 us (1%)
    psum x6, waiting for transfers between devices, broadcast(): return lax.psum(jnp.where(mine, x, jnp.zeros_like(x)), axis)  993 us
    unnamed x15, waiting for transfers between devices  425 us
    all_gather x8, blocking collectives, solve(): lax.all_gather(residual, 'col', axis=1, tiled=True)  278 us
    reduce_scatter x3, waiting for transfers between devices, solve(): lax.psum_scatter(partial_value, 'col', scatter_dimension=1, tiled=True)  223 us
    all_gather x6, blocking collectives, copy_out(): return spread(lax.all_gather(solution, 'col', axis=1, tiled=True))  198 us
  transfers between devices with their start and end apart: 12, of which 12 were waited for; matrix products, arithmetic and copies ran while one was open for 0% of the time, Pallas kernels for 0%

commit v1 on v0

v1 whole, which is shorter than its diff:
```python
import jax
import jax.numpy as jnp
from jax import lax
from jax.sharding import Mesh, PartitionSpec as P

GRID = 16
SHARD = 16
XS = 4
HS = 4
NRHS = 512
COL = ("zl", "y")
ROW = ("x", "zh")
PLANE = ROW + COL
PARTS = 1
WIDE = NRHS // PARTS
STAGED = True


def dot(a, b):
    return jnp.dot(a, b, precision=lax.Precision.HIGH)


def gather(chunk, axes, size):
    spread = jnp.broadcast_to(chunk[None], (size,) + chunk.shape)
    return lax.all_to_all(spread, axes, 0, 0, tiled=True)


def gather_down(chunk):
    width = chunk.shape[1]
    if STAGED:
        part = gather(chunk, "zh", HS).reshape(HS * chunk.shape[0], width)
        return gather(part, "x", XS).reshape(GRID * chunk.shape[0], width)
    return gather(chunk, ROW, GRID).reshape(GRID * chunk.shape[0], width)


def turn(chunk):
    return lax.ppermute(chunk, PLANE, [(r * GRID + c, c * GRID + r) for r in range(GRID) for c in range(GRID)])


def reduce_row(partial):
    chunks = lax.all_to_all(partial.reshape(GRID, SHARD, partial.shape[1]), COL, 0, 0, tiled=True)
    return jnp.sum(chunks, axis=0)


def on_device(
    rhs_sub,
    rhs_top,
    lower_inv_sub,
    lower_inv_top,
    upper_inv_sub,
    upper_inv_top,
    lower_sub,
    lower_top,
    upper_sub,
    upper_top,
    block_pattern,
):
    row = lax.axis_index(ROW)
    col = lax.axis_index(COL)
    mine = (row == col).astype(jnp.float32)
    first_layer = (lax.axis_index("layer") == 0).astype(jnp.float32)

    def block(array, kind, pair):
        return array[0, pair, 0, 0, 0, 0] * block_pattern[0, kind, pair, 0, 0, 0, 0].astype(jnp.float32)

    lower_inv = jnp.concatenate([lower_inv_sub[0, :, 0, 0], lower_inv_top[:, 0]])
    upper_inv = jnp.concatenate([upper_inv_sub[0, :, 0, 0], upper_inv_top[:, 0]])
    row_at = lax.broadcasted_iota(jnp.int32, (4, SHARD, 256), 1) + col * SHARD
    col_at = lax.broadcasted_iota(jnp.int32, (4, SHARD, 256), 2)
    packed = gather(jnp.where(col_at < row_at, lower_inv, upper_inv), COL, GRID)
    packed = packed.reshape(GRID, 4, SHARD, 256)
    down = lax.broadcasted_iota(jnp.int32, (256, 256), 0)
    across = lax.broadcasted_iota(jnp.int32, (256, 256), 1)
    unit = jnp.where(down == across, 1.0, 0.0)
    whole = [packed[:, k].reshape(256, 256) for k in range(4)]
    lower = [jnp.where(across < down, m, unit) for m in whole]
    upper = [jnp.where(across >= down, m, 0.0) for m in whole]
    top = dot(upper[3], lower[3])

    def columns(matrix):
        return lax.dynamic_slice(matrix, (0, col * SHARD), (256, SHARD))

    start = jnp.concatenate([lower_inv_sub[0, 0, 0, 0], rhs_sub[0, 0, 0, 0]], axis=1)
    start = gather_down(turn(start))
    inverse0 = start[:, :256]

    own1 = columns(lower[1])
    own2 = columns(lower[2])
    own3 = columns(top) * first_layer
    low10 = dot(lower[1], block(lower_sub, 0, 0))
    low20 = dot(lower[2], block(lower_sub, 0, 1))
    low21 = dot(lower[2], block(lower_sub, 0, 2))
    top0 = dot(top, block(lower_top, 1, 0))
    top1 = dot(top, block(lower_top, 1, 1))
    top2 = dot(top, block(lower_top, 1, 2))
    up23 = dot(upper[2], block(upper_top, 3, 2))
    up13 = dot(upper[1], block(upper_top, 3, 1))
    up03 = dot(upper[0], block(upper_top, 3, 0))
    up12 = dot(upper[1], block(upper_sub, 2, 2))
    up02 = dot(upper[0], block(upper_sub, 2, 1))
    up01 = dot(upper[0], block(upper_sub, 2, 0))
    diag2 = upper[2] * mine
    diag1 = upper[1] * mine
    diag0 = upper[0] * mine

    parts = range(PARTS)

    def share(array):
        return [array[:, p * WIDE:(p + 1) * WIDE] for p in parts]

    def each(function, *lists):
        return [function(*items) for items in zip(*lists)]

    y0 = each(lambda v: dot(inverse0, v), share(start[:, 256:]))

    y1 = each(lambda r, a: reduce_row(dot(own1, r) - dot(low10, a)), share(rhs_sub[0, 1, 0, 0]), y0)
    share2 = each(lambda r, a: dot(own2, r) - dot(low20, a), share(rhs_sub[0, 2, 0, 0]), y0)
    share3 = each(lambda r, a: dot(own3, r) - dot(top0, a), share(rhs_top[0, 0]), y0)
    y1 = each(gather_down, each(turn, y1))
    y2 = each(lambda s, a: reduce_row(s - dot(low21, a)), share2, y1)
    share3 = each(lambda s, a: s - dot(top1, a), share3, y1)
    y2 = each(gather_down, each(turn, y2))

    def swap(v):
        return lax.ppermute(v, "layer", [(0, 1), (1, 0)])

    def across_layers(chunk):
        return chunk + swap(chunk)

    final3 = each(lambda s, a: across_layers(reduce_row(s - dot(top2, a))), share3, y2)
    share2 = each(lambda a: dot(diag2, a), y2)
    share1 = each(lambda a: dot(diag1, a), y1)
    share0 = each(lambda a: dot(diag0, a), y0)
    x3 = each(gather_down, each(turn, final3))

    final2 = each(lambda s, a: reduce_row(s - dot(up23, a)), share2, x3)
    share1 = each(lambda s, a: s - dot(up13, a), share1, x3)
    share0 = each(lambda s, a: s - dot(up03, a), share0, x3)
    x2 = each(gather_down, each(turn, final2))
    final1 = each(lambda s, a: reduce_row(s - dot(up12, a)), share1, x2)
    share0 = each(lambda s, a: s - dot(up02, a), share0, x2)
    x1 = each(gather_down, each(turn, final1))
    final0 = each(lambda s, a: reduce_row(s - dot(up01, a)), share0, x1)

    solution_sub = jnp.stack([jnp.concatenate(v, axis=1) for v in (final0, final1, final2)])
    solution_top = jnp.concatenate(final3, axis=1)
    return solution_sub[None, :, None, None], solution_top[None, None]


def solution(mesh):
    fine = Mesh(mesh.devices.reshape(2, 4, 4, 2, 8), ("layer",) + PLANE)
    vector = P("layer", None, None, ROW, COL, None)
    vector_top = P(None, ROW, COL, None)
    blocks = P("layer", None, None, ROW, None, COL, None, None)
    pattern = P("layer", None, None, None, ROW, None, COL)
    placed = (vector, vector_top, vector, vector_top, vector, vector_top, blocks, blocks, blocks, blocks, pattern)
    return jax.shard_map(on_device, mesh=fine, in_specs=placed, out_specs=(vector, vector_top), check_vma=False)
```

time: 2190 us -> 402 us (0.18)
  waiting for transfers between devices: 1640 us -> 142 us
  blocking collectives: 480 us -> 76.3 us
  starting transfers between devices: 0.68 us -> 121 us
    psum x6 -> x0, waiting for transfers between devices: 993 us -> none  [broadcast(): return lax.psum(jnp.where(mine, x, jnp.zeros_like(x)), axis)]
    all_gather x14 -> x0, blocking collectives: 476 us -> none  [the longest x8 278 us: solve(): lax.all_gather(residual, 'col', axis=1, tiled=True)]
    unnamed x15 -> x0, waiting for transfers between devices: 425 us -> none
    reduce_scatter x3 -> x0, waiting for transfers between devices: 223 us -> none  [solve(): lax.psum_scatter(partial_value, 'col', scatter_dimension=1, tiled=True)]
    all_to_all x0 -> x15, waiting for transfers between devices: none -> 111 us  [the longest x12 83.9 us: gather(): return lax.all_to_all(spread, axes, 0, 0, tiled=True)]
    all_to_all x0 -> x15, starting transfers between devices: none -> 77 us  [the longest x12 57.6 us: gather(): return lax.all_to_all(spread, axes, 0, 0, tiled=True)]
    all_to_all x0 -> x4, blocking collectives: none -> 76.3 us  [the longest x3 54.3 us: reduce_row(): lax.all_to_all(partial.reshape(GRID, SHARD, partial.shape[1]), COL, 0, 0,...]
    ppermute x0 -> x7, starting transfers between devices: none -> 44 us  [the longest x6 42.1 us: turn(): lax.ppermute(chunk, PLANE, [(r * GRID + c, c * GRID + r) for r in range(G...]
  transfers between devices with their start and end apart: 12 -> 22, of which waited for: 12 -> 22; matrix products, arithmetic and copies ran while one was open for 0% -> 6% of each run, Pallas kernels for 0% -> 0%
where the time goes in v1:
time: 402 us; the launch traced here: 398 us
  waiting for transfers between devices  142 us (35%)
  starting transfers between devices  121 us (30%)
  blocking collectives  76.3 us (19%)
  matrix products  33.3 us (8%)
  local copies, waits for them, and re-layouts  14.3 us (4%)
  between operations  8.58 us (2%)
    all_to_all x12, waiting for transfers between devices, gather(): return lax.all_to_all(spread, axes, 0, 0, tiled=True)  83.9 us
    all_to_all x12, starting transfers between devices, gather(): return lax.all_to_all(spread, axes, 0, 0, tiled=True)  57.6 us
    all_to_all x3, blocking collectives, reduce_row(): lax.all_to_all(partial.reshape(GRID, SHARD, partial.shape[1]), COL, 0, 0,...  54.3 us
    ppermute x6, starting transfers between devices, turn(): lax.ppermute(chunk, PLANE, [(r * GRID + c, c * GRID + r) for r in range(G...  42.1 us
    dot_general x32, matrix products, dot(): return jnp.dot(a, b, precision=lax.Precision.HIGH)  33.3 us
    ppermute x6, waiting for transfers between devices, turn(): lax.ppermute(chunk, PLANE, [(r * GRID + c, c * GRID + r) for r in range(G...  29.5 us
    all_to_all x3, waiting for transfers between devices, reduce_row(): lax.all_to_all(partial.reshape(GRID, SHARD, partial.shape[1]), COL, 0, 0,...  27 us
    all_to_all x1, blocking collectives, gather(): return lax.all_to_all(spread, axes, 0, 0, tiled=True)  22 us
  transfers between devices with their start and end apart: 22, of which 22 were waited for; matrix products, arithmetic and copies ran while one was open for 6% of the time, Pallas kernels for 0%

profile of v1, /device:TPU:6, one launch (start us, length us, event | category | flops | bytes accessed | tf_op | source)
XLA Modules:
  0.0 397.9 jit_solution(16267721668563922876)
XLA Ops:
  1.5 9.4 %collective-permute-start = (f32[16,768]{1,0:T(8,128)S(1)}, f32[16,768]{1,0:T(8,128)S(1)}, u32[]{:S(2)}, u32[]{:S(2)}) collective-permute-start(f32[16,768]{1,0:T(8,128)S(1)} %pad_maximum_fusion), channel_id=1, source_target_pairs={{0,0},{1,16},{2,32},{3,48},{4,64},{5,80},{6,96},{7,112},{8,128},{9... | collective-permute-start | bytes 147464 | tf_op jit(solution)/shard_map/ppermute | solution.py:37
  10.9 3.4 collective-permute-done
  14.4 22.0 %all_to_all.95 = f32[4,16,768]{2,1,0:T(8,128)S(1)} all-to-all(f32[4,16,768]{2,1,0:T(8,128)S(1)} %broadcast_in_dim.109), channel_id=1, replica_groups=mesh['layer'=2,'x'=4,'zh'=4,'zl'=2,'y'=8] {'zh'}, dimensions={0} | all-to-all | bytes 393216 | tf_op jit(solution)/shard_map/all_to_all | solution.py:25
  37.4 4.6 %all-to-all-start.2 = ((f32[4,64,768]{2,1,0:T(8,128)}), f32[4,64,768]{2,1,0:T(8,128)S(1)}, u32[]{:S(2)}, u32[]{:S(2)}) async-start(f32[4,64,768]{2,1,0:T(8,128)} %broadcast_in_dim.111), calls=%async_computation.2 | async-start | bytes 1572864 | tf_op jit(solution)/shard_map/all_to_all | solution.py:25
  42.8 6.6 %all-to-all-done.2 = f32[4,64,768]{2,1,0:T(8,128)S(1)} async-done(((f32[4,64,768]{2,1,0:T(8,128)}), f32[4,64,768]{2,1,0:T(8,128)S(1)}, u32[]{:S(2)}, u32[]{:S(2)}) %all-to-all-start.2) | async-done | bytes 786464 | tf_op jit(solution)/shard_map/all_to_all | solution.py:25
  50.5 11.6 %all-to-all-start = ((f32[16,4,16,256]{3,2,1,0:T(8,128)}), f32[16,4,16,256]{3,2,1,0:T(8,128)S(1)}, u32[]{:S(2)}, u32[]{:S(2)}) async-start(f32[16,4,16,256]{3,2,1,0:T(8,128)} %broadcast_in_dim.107), calls=%async_computation | async-start | bytes 2097152 | tf_op jit(solution)/shard_map/all_to_all | solution.py:25
  65.3 19.0 %all-to-all-done = f32[16,4,16,256]{3,2,1,0:T(8,128)S(1)} async-done(((f32[16,4,16,256]{3,2,1,0:T(8,128)}), f32[16,4,16,256]{3,2,1,0:T(8,128)S(1)}, u32[]{:S(2)}, u32[]{:S(2)}) %all-to-all-start) | async-done | bytes 1048608 | tf_op jit(solution)/shard_map/all_to_all | solution.py:25
  85.4 1.2 fusion.22
  87.6 1.2 convolution_subtract_fusion.1
  88.8 17.9 %all_to_all.96 = f32[16,16,512]{2,1,0:T(8,128)S(1)} all-to-all(f32[16,16,512]{2,1,0:T(8,128)S(1)} %bitcast.168), channel_id=1, replica_groups=mesh['layer'=2,'x'=4,'zh'=4,'zl'=2,'y'=8] {'zl','y'}, dimensions={0} | all-to-all | bytes 1048576 | tf_op jit(solution)/shard_map/all_to_all | solution.py:41
  106.8 6.6 %collective-permute-start.1 = (f32[16,512]{1,0:T(8,128)S(1)}, f32[16,512]{1,0:T(8,128)S(1)}, u32[]{:S(2)}, u32[]{:S(2)}) collective-permute-start(f32[16,512]{1,0:T(8,128)S(1)} %reduce_sum.54), channel_id=1, source_target_pairs={{0,0},{1,16},{2,32},{3,48},{4,64},{5,80},{6,96},{7,112},{8,128},{9... | collective-permute-start | bytes 98312 | tf_op jit(solution)/shard_map/ppermute | solution.py:37
  114.7 4.8 %collective-permute-done.1 = f32[16,512]{1,0:T(8,128)S(1)} collective-permute-done((f32[16,512]{1,0:T(8,128)S(1)}, f32[16,512]{1,0:T(8,128)S(1)}, u32[]{:S(2)}, u32[]{:S(2)}) %collective-permute-start.1) | collective-permute-done | bytes 32800 | tf_op jit(solution)/shard_map/ppermute | solution.py:37
  120.2 3.3 all-to-all-start.4
  123.5 1.9 fusion.16
  125.4 6.8 %all-to-all-done.4 = f32[4,16,512]{2,1,0:T(8,128)S(1)} async-done(((f32[4,16,512]{2,1,0:T(8,128)}), f32[4,16,512]{2,1,0:T(8,128)S(1)}, u32[]{:S(2)}, u32[]{:S(2)}) %all-to-all-start.4) | async-done | bytes 131104 | tf_op jit(solution)/shard_map/all_to_all | solution.py:25
  133.0 4.5 %all-to-all-start.5 = ((f32[4,64,512]{2,1,0:T(8,128)}), f32[4,64,512]{2,1,0:T(8,128)S(1)}, u32[]{:S(2)}, u32[]{:S(2)}) async-start(f32[4,64,512]{2,1,0:T(8,128)} %broadcast_in_dim.117), calls=%async_computation.5 | async-start | bytes 1048576 | tf_op jit(solution)/shard_map/all_to_all | solution.py:25
  137.5 1.2 fusion.18
  139.2 4.4 %all-to-all-done.5 = f32[4,64,512]{2,1,0:T(8,128)S(1)} async-done(((f32[4,64,512]{2,1,0:T(8,128)}), f32[4,64,512]{2,1,0:T(8,128)S(1)}, u32[]{:S(2)}, u32[]{:S(2)}) %all-to-all-start.5) | async-done | bytes 524320 | tf_op jit(solution)/shard_map/all_to_all | solution.py:25
  143.6 1.4 fusion.96
  145.0 2.0 fusion.2
  147.0 6.8 %all-to-all-start.6 = ((f32[16,16,512]{2,1,0:T(8,128)}), f32[16,16,512]{2,1,0:T(8,128)S(1)}, u32[]{:S(2)}, u32[]{:S(2)}) async-start(f32[16,16,512]{2,1,0:T(8,128)} %bitcast.36), calls=%async_computation.6 | async-start | bytes 1048576 | tf_op jit(solution)/shard_map/all_to_all | solution.py:41
  155.9 1.3 fusion.26
  157.3 8.1 %all-to-all-done.6 = f32[16,16,512]{2,1,0:T(8,128)S(1)} async-done(((f32[16,16,512]{2,1,0:T(8,128)}), f32[16,16,512]{2,1,0:T(8,128)S(1)}, u32[]{:S(2)}, u32[]{:S(2)}) %all-to-all-start.6) | async-done | bytes 524320 | tf_op jit(solution)/shard_map/all_to_all | solution.py:41
  165.4 6.5 %collective-permute-start.2 = (f32[16,512]{1,0:T(8,128)S(1)}, f32[16,512]{1,0:T(8,128)S(1)}, u32[]{:S(2)}, u32[]{:S(2)}) collective-permute-start(f32[16,512]{1,0:T(8,128)S(1)} %reduce_sum.55), channel_id=1, source_target_pairs={{0,0},{1,16},{2,32},{3,48},{4,64},{5,80},{6,96},{7,112},{8,128},{9... | collective-permute-start | bytes 98312 | tf_op jit(solution)/shard_map/ppermute | solution.py:37
  172.3 5.8 %collective-permute-done.2 = f32[16,512]{1,0:T(8,128)S(1)} collective-permute-done((f32[16,512]{1,0:T(8,128)S(1)}, f32[16,512]{1,0:T(8,128)S(1)}, u32[]{:S(2)}, u32[]{:S(2)}) %collective-permute-start.2) | collective-permute-done | bytes 32800 | tf_op jit(solution)/shard_map/ppermute | solution.py:37
  178.8 3.5 all-to-all-start.7
  182.3 1.3 fusion.20
  183.6 7.2 %all-to-all-done.7 = f32[4,16,512]{2,1,0:T(8,128)S(1)} async-done(((f32[4,16,512]{2,1,0:T(8,128)}), f32[4,16,512]{2,1,0:T(8,128)S(1)}, u32[]{:S(2)}, u32[]{:S(2)}) %all-to-all-start.7) | async-done | bytes 131104 | tf_op jit(solution)/shard_map/all_to_all | solution.py:25
  191.6 4.5 %all-to-all-start.8 = ((f32[4,64,512]{2,1,0:T(8,128)}), f32[4,64,512]{2,1,0:T(8,128)S(1)}, u32[]{:S(2)}, u32[]{:S(2)}) async-start(f32[4,64,512]{2,1,0:T(8,128)} %broadcast_in_dim.120), calls=%async_computation.8 | async-start | bytes 1048576 | tf_op jit(solution)/shard_map/all_to_all | solution.py:25
  196.1 1.3 fusion.24
  197.5 1.2 fusion.94
  198.7 3.5 all-to-all-done.8
  203.7 18.2 %all_to_all.97 = f32[16,16,512]{2,1,0:T(8,128)S(1)} all-to-all(f32[16,16,512]{2,1,0:T(8,128)S(1)} %bitcast.169), channel_id=1, replica_groups=mesh['layer'=2,'x'=4,'zh'=4,'zl'=2,'y'=8] {'zl','y'}, dimensions={0} | all-to-all | bytes 1048576 | tf_op jit(solution)/shard_map/all_to_all | solution.py:41
  221.9 1.9 collective-permute-start.3
  225.0 6.6 %collective-permute-start.4 = (f32[16,512]{1,0:T(8,128)S(1)}, f32[16,512]{1,0:T(8,128)S(1)}, u32[]{:S(2)}, u32[]{:S(2)}) collective-permute-start(f32[16,512]{1,0:T(8,128)S(1)} %add.63), channel_id=1, source_target_pairs={{0,0},{1,16},{2,32},{3,48},{4,64},{5,80},{6,96},{7,112},{8,128},{9... | collective-permute-start | bytes 98312 | tf_op jit(solution)/shard_map/ppermute | solution.py:37
  231.7 6.1 %collective-permute-done.4 = f32[16,512]{1,0:T(8,128)S(1)} collective-permute-done((f32[16,512]{1,0:T(8,128)S(1)}, f32[16,512]{1,0:T(8,128)S(1)}, u32[]{:S(2)}, u32[]{:S(2)}) %collective-permute-start.4) | collective-permute-done | bytes 32800 | tf_op jit(solution)/shard_map/ppermute | solution.py:37
  238.4 4.6 %all-to-all-start.10 = ((f32[4,16,512]{2,1,0:T(8,128)}), f32[4,16,512]{2,1,0:T(8,128)S(1)}, u32[]{:S(2)}, u32[]{:S(2)}) async-start(f32[4,16,512]{2,1,0:T(8,128)} %broadcast_in_dim.121), calls=%async_computation.10 | async-start | bytes 262144 | tf_op jit(solution)/shard_map/all_to_all | solution.py:25
  243.5 8.5 %all-to-all-done.10 = f32[4,16,512]{2,1,0:T(8,128)S(1)} async-done(((f32[4,16,512]{2,1,0:T(8,128)}), f32[4,16,512]{2,1,0:T(8,128)S(1)}, u32[]{:S(2)}, u32[]{:S(2)}) %all-to-all-start.10) | async-done | bytes 131104 | tf_op jit(solution)/shard_map/all_to_all | solution.py:25
  252.9 4.6 %all-to-all-start.11 = ((f32[4,64,512]{2,1,0:T(8,128)}), f32[4,64,512]{2,1,0:T(8,128)S(1)}, u32[]{:S(2)}, u32[]{:S(2)}) async-start(f32[4,64,512]{2,1,0:T(8,128)} %broadcast_in_dim.123), calls=%async_computation.11 | async-start | bytes 1048576 | tf_op jit(solution)/shard_map/all_to_all | solution.py:25
  257.5 2.0 fusion.12
  259.9 3.6 all-to-all-done.11
  263.5 2.1 convolution_subtract_fusion.7
  265.7 6.2 %all-to-all-start.12 = ((f32[16,16,512]{2,1,0:T(8,128)}), f32[16,16,512]{2,1,0:T(8,128)S(1)}, u32[]{:S(2)}, u32[]{:S(2)}) async-start(f32[16,16,512]{2,1,0:T(8,128)} %bitcast.48), calls=%async_computation.12 | async-start | bytes 1048576 | tf_op jit(solution)/shard_map/all_to_all | solution.py:41
  273.2 11.6 %all-to-all-done.12 = f32[16,16,512]{2,1,0:T(8,128)S(1)} async-done(((f32[16,16,512]{2,1,0:T(8,128)}), f32[16,16,512]{2,1,0:T(8,128)S(1)}, u32[]{:S(2)}, u32[]{:S(2)}) %all-to-all-start.12) | async-done | bytes 524320 | tf_op jit(solution)/shard_map/all_to_all | solution.py:41
  284.8 6.6 %collective-permute-start.5 = (f32[16,512]{1,0:T(8,128)S(1)}, f32[16,512]{1,0:T(8,128)S(1)}, u32[]{:S(2)}, u32[]{:S(2)}) collective-permute-start(f32[16,512]{1,0:T(8,128)S(1)} %reduce_sum.57), channel_id=1, source_target_pairs={{0,0},{1,16},{2,32},{3,48},{4,64},{5,80},{6,96},{7,112},{8,128},{9... | collective-permute-start | bytes 98312 | tf_op jit(solution)/shard_map/ppermute | solution.py:37
  291.3 1.2 fusion.8
  292.6 4.9 %collective-permute-done.5 = f32[16,512]{1,0:T(8,128)S(1)} collective-permute-done((f32[16,512]{1,0:T(8,128)S(1)}, f32[16,512]{1,0:T(8,128)S(1)}, u32[]{:S(2)}, u32[]{:S(2)}) %collective-permute-start.5) | collective-permute-done | bytes 32800 | tf_op jit(solution)/shard_map/ppermute | solution.py:37
  298.2 3.9 all-to-all-start.13
  302.1 1.2 fusion.6
  303.3 7.8 %all-to-all-done.13 = f32[4,16,512]{2,1,0:T(8,128)S(1)} async-done(((f32[4,16,512]{2,1,0:T(8,128)}), f32[4,16,512]{2,1,0:T(8,128)S(1)}, u32[]{:S(2)}, u32[]{:S(2)}) %all-to-all-start.13) | async-done | bytes 131104 | tf_op jit(solution)/shard_map/all_to_all | solution.py:25
  312.0 4.5 %all-to-all-start.14 = ((f32[4,64,512]{2,1,0:T(8,128)}), f32[4,64,512]{2,1,0:T(8,128)S(1)}, u32[]{:S(2)}, u32[]{:S(2)}) async-start(f32[4,64,512]{2,1,0:T(8,128)} %broadcast_in_dim.126), calls=%async_computation.14 | async-start | bytes 1048576 | tf_op jit(solution)/shard_map/all_to_all | solution.py:25
  317.3 5.2 %all-to-all-done.14 = f32[4,64,512]{2,1,0:T(8,128)S(1)} async-done(((f32[4,64,512]{2,1,0:T(8,128)}), f32[4,64,512]{2,1,0:T(8,128)S(1)}, u32[]{:S(2)}, u32[]{:S(2)}) %all-to-all-start.14) | async-done | bytes 524320 | tf_op jit(solution)/shard_map/all_to_all | solution.py:25
  323.7 6.4 %all-to-all-start.15 = ((f32[16,16,512]{2,1,0:T(8,128)}), f32[16,16,512]{2,1,0:T(8,128)S(1)}, u32[]{:S(2)}, u32[]{:S(2)}) async-start(f32[16,16,512]{2,1,0:T(8,128)} %bitcast.59), calls=%async_computation.15 | async-start | bytes 1048576 | tf_op jit(solution)/shard_map/all_to_all | solution.py:41
  332.2 1.9 fusion.28
  334.5 7.4 %all-to-all-done.15 = f32[16,16,512]{2,1,0:T(8,128)S(1)} async-done(((f32[16,16,512]{2,1,0:T(8,128)}), f32[16,16,512]{2,1,0:T(8,128)S(1)}, u32[]{:S(2)}, u32[]{:S(2)}) %all-to-all-start.15) | async-done | bytes 524320 | tf_op jit(solution)/shard_map/all_to_all | solution.py:41
  341.9 6.3 %collective-permute-start.6 = (f32[16,512]{1,0:T(8,128)S(1)}, f32[16,512]{1,0:T(8,128)S(1)}, u32[]{:S(2)}, u32[]{:S(2)}) collective-permute-start(f32[16,512]{1,0:T(8,128)S(1)} %reduce_sum.58), channel_id=1, source_target_pairs={{0,0},{1,16},{2,32},{3,48},{4,64},{5,80},{6,96},{7,112},{8,128},{9... | collective-permute-start | bytes 98312 | tf_op jit(solution)/shard_map/ppermute | solution.py:37
  348.3 1.9 fusion.14
  350.2 4.4 %collective-permute-done.6 = f32[16,512]{1,0:T(8,128)S(1)} collective-permute-done((f32[16,512]{1,0:T(8,128)S(1)}, f32[16,512]{1,0:T(8,128)S(1)}, u32[]{:S(2)}, u32[]{:S(2)}) %collective-permute-start.6) | collective-permute-done | bytes 32800 | tf_op jit(solution)/shard_map/ppermute | solution.py:37
  355.3 3.3 all-to-all-start.16
  358.6 1.9 fusion.10
  360.6 6.6 %all-to-all-done.16 = f32[4,16,512]{2,1,0:T(8,128)S(1)} async-done(((f32[4,16,512]{2,1,0:T(8,128)}), f32[4,16,512]{2,1,0:T(8,128)S(1)}, u32[]{:S(2)}, u32[]{:S(2)}) %all-to-all-start.16) | async-done | bytes 131104 | tf_op jit(solution)/shard_map/all_to_all | solution.py:25
  368.0 4.6 %all-to-all-start.17 = ((f32[4,64,512]{2,1,0:T(8,128)}), f32[4,64,512]{2,1,0:T(8,128)S(1)}, u32[]{:S(2)}, u32[]{:S(2)}) async-start(f32[4,64,512]{2,1,0:T(8,128)} %broadcast_in_dim.129), calls=%async_computation.17 | async-start | bytes 1048576 | tf_op jit(solution)/shard_map/all_to_all | solution.py:25
  374.0 4.7 %all-to-all-done.17 = f32[4,64,512]{2,1,0:T(8,128)S(1)} async-done(((f32[4,64,512]{2,1,0:T(8,128)}), f32[4,64,512]{2,1,0:T(8,128)S(1)}, u32[]{:S(2)}, u32[]{:S(2)}) %all-to-all-start.17) | async-done | bytes 524320 | tf_op jit(solution)/shard_map/all_to_all | solution.py:25
  379.1 18.2 %all_to_all.98 = f32[16,16,512]{2,1,0:T(8,128)S(1)} all-to-all(f32[16,16,512]{2,1,0:T(8,128)S(1)} %bitcast.167), channel_id=1, replica_groups=mesh['layer'=2,'x'=4,'zh'=4,'zl'=2,'y'=8] {'zl','y'}, dimensions={0} | all-to-all | bytes 1048576 | tf_op jit(solution)/shard_map/all_to_all | solution.py:41
  (82 shorter events, 25.0 us)
Async XLA Ops:
  0.6 201.9 %copy-start = (f32[1,1,16,512]{3,2,1,0:T(8,128)S(1)}, f32[1,1,16,512]{3,2,1,0:T(8,128)}, u32[]{:S(2)}) copy-start(f32[1,1,16,512]{3,2,1,0:T(8,128)} %param.12) | copy-start | bytes 98308
  0.6 0.8 copy-start.11
  1.5 12.9 %collective-permute-start = (f32[16,768]{1,0:T(8,128)S(1)}, f32[16,768]{1,0:T(8,128)S(1)}, u32[]{:S(2)}, u32[]{:S(2)}) collective-permute-start(f32[16,768]{1,0:T(8,128)S(1)} %pad_maximum_fusion), channel_id=1, source_target_pairs={{0,0},{1,16},{2,32},{3,48},{4,64},{5,80},{6,96},{7,112},{8,128},{9... | collective-permute-start | bytes 147464 | tf_op jit(solution)/shard_map/ppermute | solution.py:37
  37.4 4.6 %copy-start.12 = (f32[1,3,1,1,16,256]{5,4,3,2,1,0:T(8,128)S(1)}, f32[1,3,1,1,16,256]{5,4,3,2,1,0:T(8,128)}, u32[]{:S(2)}) copy-start(f32[1,3,1,1,16,256]{5,4,3,2,1,0:T(8,128)} %param.15) | copy-start | bytes 147460
  37.4 4.7 %copy-start.16 = (f32[1,1,16,256]{3,2,1,0:T(8,128)S(1)}, f32[1,1,16,256]{3,2,1,0:T(8,128)}, u32[]{:S(2)}) copy-start(f32[1,1,16,256]{3,2,1,0:T(8,128)} %param.16) | copy-start | bytes 49156
  37.4 12.1 %all-to-all-start.2 = ((f32[4,64,768]{2,1,0:T(8,128)}), f32[4,64,768]{2,1,0:T(8,128)S(1)}, u32[]{:S(2)}, u32[]{:S(2)}) async-start(f32[4,64,768]{2,1,0:T(8,128)} %broadcast_in_dim.111), calls=%async_computation.2 | async-start | bytes 1572864 | tf_op jit(solution)/shard_map/all_to_all | solution.py:25
  42.0 0.7 copy-start.15
  50.5 33.8 %all-to-all-start = ((f32[16,4,16,256]{3,2,1,0:T(8,128)}), f32[16,4,16,256]{3,2,1,0:T(8,128)S(1)}, u32[]{:S(2)}, u32[]{:S(2)}) async-start(f32[16,4,16,256]{3,2,1,0:T(8,128)} %broadcast_in_dim.107), calls=%async_computation | async-start | bytes 2097152 | tf_op jit(solution)/shard_map/all_to_all | solution.py:25
  62.1 0.7 copy-start.14
  86.7 1.0 copy-start.4
  106.8 12.7 %collective-permute-start.1 = (f32[16,512]{1,0:T(8,128)S(1)}, f32[16,512]{1,0:T(8,128)S(1)}, u32[]{:S(2)}, u32[]{:S(2)}) collective-permute-start(f32[16,512]{1,0:T(8,128)S(1)} %reduce_sum.54), channel_id=1, source_target_pairs={{0,0},{1,16},{2,32},{3,48},{4,64},{5,80},{6,96},{7,112},{8,128},{9... | collective-permute-start | bytes 98312 | tf_op jit(solution)/shard_map/ppermute | solution.py:37
  120.2 12.0 %all-to-all-start.4 = ((f32[4,16,512]{2,1,0:T(8,128)}), f32[4,16,512]{2,1,0:T(8,128)S(1)}, u32[]{:S(2)}, u32[]{:S(2)}) async-start(f32[4,16,512]{2,1,0:T(8,128)} %broadcast_in_dim.115), calls=%async_computation.4 | async-start | bytes 262144 | tf_op jit(solution)/shard_map/all_to_all | solution.py:25
  133.0 10.5 %all-to-all-start.5 = ((f32[4,64,512]{2,1,0:T(8,128)}), f32[4,64,512]{2,1,0:T(8,128)S(1)}, u32[]{:S(2)}, u32[]{:S(2)}) async-start(f32[4,64,512]{2,1,0:T(8,128)} %broadcast_in_dim.117), calls=%async_computation.5 | async-start | bytes 1048576 | tf_op jit(solution)/shard_map/all_to_all | solution.py:25
  143.6 1.4 copy-start.5
  143.6 1.4 copy-start.10
  147.0 18.4 %all-to-all-start.6 = ((f32[16,16,512]{2,1,0:T(8,128)}), f32[16,16,512]{2,1,0:T(8,128)S(1)}, u32[]{:S(2)}, u32[]{:S(2)}) async-start(f32[16,16,512]{2,1,0:T(8,128)} %bitcast.36), calls=%async_computation.6 | async-start | bytes 1048576 | tf_op jit(solution)/shard_map/all_to_all | solution.py:41
  165.4 12.7 %collective-permute-start.2 = (f32[16,512]{1,0:T(8,128)S(1)}, f32[16,512]{1,0:T(8,128)S(1)}, u32[]{:S(2)}, u32[]{:S(2)}) collective-permute-start(f32[16,512]{1,0:T(8,128)S(1)} %reduce_sum.55), channel_id=1, source_target_pairs={{0,0},{1,16},{2,32},{3,48},{4,64},{5,80},{6,96},{7,112},{8,128},{9... | collective-permute-start | bytes 98312 | tf_op jit(solution)/shard_map/ppermute | solution.py:37
  178.8 12.0 %all-to-all-start.7 = ((f32[4,16,512]{2,1,0:T(8,128)}), f32[4,16,512]{2,1,0:T(8,128)S(1)}, u32[]{:S(2)}, u32[]{:S(2)}) async-start(f32[4,16,512]{2,1,0:T(8,128)} %broadcast_in_dim.118), calls=%async_computation.7 | async-start | bytes 262144 | tf_op jit(solution)/shard_map/all_to_all | solution.py:25
  191.6 10.5 %all-to-all-start.8 = ((f32[4,64,512]{2,1,0:T(8,128)}), f32[4,64,512]{2,1,0:T(8,128)S(1)}, u32[]{:S(2)}, u32[]{:S(2)}) async-start(f32[4,64,512]{2,1,0:T(8,128)} %broadcast_in_dim.120), calls=%async_computation.8 | async-start | bytes 1048576 | tf_op jit(solution)/shard_map/all_to_all | solution.py:25
  202.2 1.0 copy-start.1
  221.9 3.1 collective-permute-start.3
  225.0 13.4 %copy-start.13 = (f32[16,512]{1,0:T(8,128)}, f32[16,512]{1,0:T(8,128)S(1)}, u32[]{:S(2)}) copy-start(f32[16,512]{1,0:T(8,128)S(1)} %add.63) | copy-start | bytes 98308
  225.0 12.7 %collective-permute-start.4 = (f32[16,512]{1,0:T(8,128)S(1)}, f32[16,512]{1,0:T(8,128)S(1)}, u32[]{:S(2)}, u32[]{:S(2)}) collective-permute-start(f32[16,512]{1,0:T(8,128)S(1)} %add.63), channel_id=1, source_target_pairs={{0,0},{1,16},{2,32},{3,48},{4,64},{5,80},{6,96},{7,112},{8,128},{9... | collective-permute-start | bytes 98312 | tf_op jit(solution)/shard_map/ppermute | solution.py:37
  238.4 13.6 %all-to-all-start.10 = ((f32[4,16,512]{2,1,0:T(8,128)}), f32[4,16,512]{2,1,0:T(8,128)S(1)}, u32[]{:S(2)}, u32[]{:S(2)}) async-start(f32[4,16,512]{2,1,0:T(8,128)} %broadcast_in_dim.121), calls=%async_computation.10 | async-start | bytes 262144 | tf_op jit(solution)/shard_map/all_to_all | solution.py:25
  252.9 4.6 %copy-start.6 = (f32[16,1,16,256]{3,2,1,0:T(8,128)S(1)}, f32[16,1,16,256]{3,2,1,0:T(8,128)}, u32[]{:S(2)}) copy-start(f32[16,1,16,256]{3,2,1,0:T(8,128)} %get-tuple-element.13) | copy-start | bytes 786436
  252.9 10.7 %all-to-all-start.11 = ((f32[4,64,512]{2,1,0:T(8,128)}), f32[4,64,512]{2,1,0:T(8,128)S(1)}, u32[]{:S(2)}, u32[]{:S(2)}) async-start(f32[4,64,512]{2,1,0:T(8,128)} %broadcast_in_dim.123), calls=%async_computation.11 | async-start | bytes 1048576 | tf_op jit(solution)/shard_map/all_to_all | solution.py:25
  257.5 2.0 copy-start.2
  265.7 19.1 %all-to-all-start.12 = ((f32[16,16,512]{2,1,0:T(8,128)}), f32[16,16,512]{2,1,0:T(8,128)S(1)}, u32[]{:S(2)}, u32[]{:S(2)}) async-start(f32[16,16,512]{2,1,0:T(8,128)} %bitcast.48), calls=%async_computation.12 | async-start | bytes 1048576 | tf_op jit(solution)/shard_map/all_to_all | solution.py:41
  284.8 12.7 %collective-permute-start.5 = (f32[16,512]{1,0:T(8,128)S(1)}, f32[16,512]{1,0:T(8,128)S(1)}, u32[]{:S(2)}, u32[]{:S(2)}) collective-permute-start(f32[16,512]{1,0:T(8,128)S(1)} %reduce_sum.57), channel_id=1, source_target_pairs={{0,0},{1,16},{2,32},{3,48},{4,64},{5,80},{6,96},{7,112},{8,128},{9... | collective-permute-start | bytes 98312 | tf_op jit(solution)/shard_map/ppermute | solution.py:37
  298.2 13.0 %all-to-all-start.13 = ((f32[4,16,512]{2,1,0:T(8,128)}), f32[4,16,512]{2,1,0:T(8,128)S(1)}, u32[]{:S(2)}, u32[]{:S(2)}) async-start(f32[4,16,512]{2,1,0:T(8,128)} %broadcast_in_dim.124), calls=%async_computation.13 | async-start | bytes 262144 | tf_op jit(solution)/shard_map/all_to_all | solution.py:25
  312.0 10.5 %all-to-all-start.14 = ((f32[4,64,512]{2,1,0:T(8,128)}), f32[4,64,512]{2,1,0:T(8,128)S(1)}, u32[]{:S(2)}, u32[]{:S(2)}) async-start(f32[4,64,512]{2,1,0:T(8,128)} %broadcast_in_dim.126), calls=%async_computation.14 | async-start | bytes 1048576 | tf_op jit(solution)/shard_map/all_to_all | solution.py:25
  323.7 8.4 %copy-start.3 = (f32[16,1,16,256]{3,2,1,0:T(8,128)S(1)}, f32[16,1,16,256]{3,2,1,0:T(8,128)}, u32[]{:S(2)}) copy-start(f32[16,1,16,256]{3,2,1,0:T(8,128)} %get-tuple-element.17) | copy-start | bytes 786436
  323.7 18.2 %all-to-all-start.15 = ((f32[16,16,512]{2,1,0:T(8,128)}), f32[16,16,512]{2,1,0:T(8,128)S(1)}, u32[]{:S(2)}, u32[]{:S(2)}) async-start(f32[16,16,512]{2,1,0:T(8,128)} %bitcast.59), calls=%async_computation.15 | async-start | bytes 1048576 | tf_op jit(solution)/shard_map/all_to_all | solution.py:41
  341.9 12.7 %collective-permute-start.6 = (f32[16,512]{1,0:T(8,128)S(1)}, f32[16,512]{1,0:T(8,128)S(1)}, u32[]{:S(2)}, u32[]{:S(2)}) collective-permute-start(f32[16,512]{1,0:T(8,128)S(1)} %reduce_sum.58), channel_id=1, source_target_pairs={{0,0},{1,16},{2,32},{3,48},{4,64},{5,80},{6,96},{7,112},{8,128},{9... | collective-permute-start | bytes 98312 | tf_op jit(solution)/shard_map/ppermute | solution.py:37
  355.3 11.8 %all-to-all-start.16 = ((f32[4,16,512]{2,1,0:T(8,128)}), f32[4,16,512]{2,1,0:T(8,128)S(1)}, u32[]{:S(2)}, u32[]{:S(2)}) async-start(f32[4,16,512]{2,1,0:T(8,128)} %broadcast_in_dim.127), calls=%async_computation.16 | async-start | bytes 262144 | tf_op jit(solution)/shard_map/all_to_all | solution.py:25
  368.0 4.6 %copy-start.7 = (f32[256,256]{1,0:T(8,128)S(1)}, f32[256,256]{1,0:T(8,128)}, u32[]{:S(2)}) copy-start(f32[256,256]{1,0:T(8,128)} %fusion.28) | copy-start | bytes 786436
  368.0 10.7 %all-to-all-start.17 = ((f32[4,64,512]{2,1,0:T(8,128)}), f32[4,64,512]{2,1,0:T(8,128)S(1)}, u32[]{:S(2)}, u32[]{:S(2)}) async-start(f32[4,64,512]{2,1,0:T(8,128)} %broadcast_in_dim.129), calls=%async_computation.17 | async-start | bytes 1048576 | tf_op jit(solution)/shard_map/all_to_all | solution.py:25
  372.6 1.0 copy-start.8
  373.6 5.1 %copy-start.9 = (f32[256,256]{1,0:T(8,128)S(1)}, f32[256,256]{1,0:T(8,128)}, u32[]{:S(2)}) copy-start(f32[256,256]{1,0:T(8,128)} %fusion.10) | copy-start | bytes 786436

commit v2 on v1

v2 whole, which is shorter than its diff:
```python
import jax
import jax.numpy as jnp
from jax import lax
from jax.sharding import Mesh, PartitionSpec as P


W = 256
HALF = 256
GRID = 16
SHARD = 16
YS = 8
CHUNK = 2 * SHARD
COL = ("zl", "y")
ROW = ("x", "zh")
PLANE = ROW + COL
SWAP = [(0, 1), (1, 0)]
NEAR = (
    (6, 7, 3, 4, 0, 1, 5, 2),
    (3, 7, 4, 0, 5, 1, 2, 6),
    (1, 0, 4, 5, 7, 6, 2, 3),
    (0, 2, 4, 5, 1, 6, 7, 3),
    (4, 0, 5, 6, 2, 1, 3, 7),
    (1, 5, 4, 6, 2, 3, 7, 0),
    (5, 2, 6, 7, 3, 1, 0, 4),
    (2, 6, 3, 7, 4, 0, 5, 1),
)
PLAIN = tuple(tuple(range(YS)) for _ in range(YS))


def dot(a, b):
    return jnp.dot(a, b, precision=lax.Precision.HIGH)


def turn(chunk, table):
    pairs = []
    for r in range(GRID):
        for zl in range(2):
            for y in range(YS):
                target = (r // YS) * YS + table[r % YS][y]
                pairs.append((r * GRID + zl * YS + y, target * GRID + zl * YS + r % YS))
    return lax.ppermute(chunk, PLANE, pairs)


def gather(chunk, axes, size):
    return lax.all_to_all(jnp.broadcast_to(chunk[None], (size,) + chunk.shape), axes, 0, 0, tiled=True)


def gather_down(chunk):
    return gather(chunk, ROW, GRID).reshape(GRID * chunk.shape[0], chunk.shape[1])


def reduce_row(partial):
    return jnp.sum(lax.all_to_all(partial.reshape(YS, CHUNK, partial.shape[1]), "y", 0, 0, tiled=True), axis=0)


def reduce_layers(partial):
    halves = partial.reshape(W, 2, HALF // 2).transpose(1, 0, 2)
    return jnp.sum(lax.all_to_all(halves, "layer", 0, 0, tiled=True), axis=0)


def gather_layers(part):
    return gather(part, "layer", 2).transpose(1, 0, 2).reshape(part.shape[0], HALF)


def on_device(
    rhs_sub,
    rhs_top,
    lower_inv_sub,
    lower_inv_top,
    upper_inv_sub,
    upper_inv_top,
    lower_sub,
    lower_top,
    upper_sub,
    upper_top,
    block_pattern,
):
    layer = lax.axis_index("layer")
    row = lax.axis_index(ROW)
    col = lax.axis_index(COL)
    y_at = lax.axis_index("y")
    even = lax.axis_index("zl") == 0

    def ordered(own, other, axis, first=even):
        return jnp.where(first, jnp.concatenate([own, other], axis), jnp.concatenate([other, own], axis))

    lower_inv = jnp.concatenate([lower_inv_sub[0, :, 0, 0], lower_inv_top[:, 0]])
    upper_inv = jnp.concatenate([upper_inv_sub[0, :, 0, 0], upper_inv_top[:, 0]])
    row_at = lax.broadcasted_iota(jnp.int32, (4, SHARD, W), 1) + col * SHARD
    col_at = lax.broadcasted_iota(jnp.int32, (4, SHARD, W), 2)
    packed = gather(jnp.where(col_at < row_at, lower_inv, upper_inv), COL, GRID)

    rhs = jnp.concatenate([rhs_sub[0, :, 0, 0], rhs_top[:, 0]])
    keep = jnp.where(even, rhs[:, :, :HALF], rhs[:, :, HALF:])
    send = jnp.where(even, rhs[:, :, HALF:], rhs[:, :, :HALF])
    got = lax.ppermute(jnp.concatenate([send, lower_inv_sub[0, :1, 0, 0]]), "zl", SWAP)
    rhs = ordered(keep, got[:4], 1)
    start = jnp.concatenate([ordered(lower_inv_sub[0, 0, 0, 0], got[4], 0), rhs[0]], axis=1)
    start = turn(start, PLAIN)
    start = gather_down(start)

    def masked(array, kind):
        return array[0, :, 0, 0, 0, 0] * block_pattern[0, kind, :, 0, 0, 0, 0].astype(jnp.float32)[:, None, None]

    def both(own):
        other = lax.ppermute(own, "zl", SWAP)
        return [ordered(own[pair], other[pair], 1) for pair in range(own.shape[0])]

    low_own = masked(lower_sub, 0)
    low_sub = both(low_own[:1]) + both(low_own[1:])
    low_top = both(masked(lower_top, 1))
    up_top = both(masked(upper_top, 3))
    up_sub = both(masked(upper_sub, 2))

    packed = packed.reshape(GRID, 4, SHARD, W)
    natural = lax.broadcasted_iota(jnp.int32, (W, W), 0)
    across = lax.broadcasted_iota(jnp.int32, (W, W), 1)
    table = jnp.array(NEAR, jnp.int32)
    mine = lax.dynamic_index_in_dim(table, row % YS, 0, keepdims=False)
    slot = natural // CHUNK
    moved = natural % CHUNK
    for y in range(YS):
        moved = moved + jnp.where(slot == y, mine[y] * CHUNK, 0)
    pick = (across == moved).astype(jnp.float32)
    whole = [packed[:, k].reshape(W, W) for k in range(4)]
    near = [None] + [jnp.dot(pick, whole[k], precision=lax.Precision.HIGHEST) for k in (1, 2, 3)]

    def lower_of(matrix, down):
        return jnp.where(across < down, matrix, jnp.where(across == down, 1.0, 0.0))

    def upper_of(matrix, down):
        return jnp.where(across >= down, matrix, 0.0)

    lower1 = lower_of(near[1], moved)
    lower2 = lower_of(near[2], moved)
    top = dot(upper_of(near[3], moved), lower_of(whole[3], natural))
    upper2 = upper_of(near[2], moved)
    upper1 = upper_of(near[1], moved)
    upper0 = upper_of(whole[0], natural)
    upper0 = upper0.reshape(2, YS, SHARD, W).transpose(1, 0, 2, 3).reshape(W, W)

    def columns(matrix):
        left = lax.dynamic_slice(matrix, (0, y_at * SHARD), (W, SHARD))
        right = lax.dynamic_slice(matrix, (0, W // 2 + y_at * SHARD), (W, SHARD))
        return jnp.concatenate([left, right], axis=1)

    low10 = dot(lower1, low_sub[0])
    share1 = dot(columns(lower1), rhs[1])
    share2 = dot(columns(lower2), rhs[2])
    share3 = dot(columns(top), rhs[3]) * (layer == 0).astype(jnp.float32)

    own_column = (row % YS == y_at).astype(jnp.float32)
    diag2 = upper2 * own_column
    diag1 = upper1 * own_column
    diag0 = upper0 * own_column

    def own(pair):
        return jnp.where(row < YS, pair[:W], pair[W:])

    start = start.reshape(2, YS, 2, SHARD, W + HALF).transpose(0, 2, 1, 3, 4).reshape(2, W, W + HALF)
    y0 = jnp.concatenate([dot(start[s, :, :W], start[s, :, W:]) for s in range(2)])

    y1 = reduce_row(share1 - dot(low10, y0))
    y1 = turn(y1, NEAR)
    low20 = dot(lower2, low_sub[1])
    low21 = dot(lower2, low_sub[2])
    share2 = share2 - dot(low20, y0)
    y1 = gather_down(y1)

    y2 = reduce_row(share2 - dot(low21, y1))
    y2 = turn(y2, NEAR)
    share3 = share3 - dot(dot(top, low_top[0]), y0)
    share3 = share3 - dot(dot(top, low_top[1]), y1)
    top2 = dot(top, low_top[2])
    y2 = gather_down(y2)

    x3 = reduce_layers(share3 - dot(top2, y2))
    final3 = reduce_row(x3)
    x3 = turn(final3, NEAR)
    back0 = dot(diag0, own(y0))
    back1 = dot(diag1, own(y1))
    back2 = dot(diag2, own(y2))
    up23 = dot(upper2, up_top[2])
    x3 = gather_down(x3)
    x3 = gather_layers(x3)
    final3 = ordered(final3, lax.ppermute(final3, "layer", SWAP), 1, layer == 0)

    final2 = reduce_row(back2 - dot(up23, x3))
    x2 = turn(final2, NEAR)
    up12 = dot(upper1, up_sub[2])
    back1 = back1 - dot(dot(upper1, up_top[1]), x3)
    back0 = back0 - dot(dot(upper0, up_top[0]), x3)
    x2 = gather_down(x2)

    final1 = reduce_row(back1 - dot(up12, x2))
    x1 = turn(final1, NEAR)
    up01 = dot(upper0, up_sub[0])
    back0 = back0 - dot(dot(upper0, up_sub[1]), x2)
    x1 = gather_down(x1)

    final0 = reduce_row(back0 - dot(up01, x1))

    solved = jnp.stack([final1, final2, final3])
    upper_rows, lower_rows = solved[:, :SHARD], solved[:, SHARD:]
    straight, crossed = [], []
    for r in range(GRID):
        for zl in range(2):
            for y in range(YS):
                target = r * GRID + 2 * NEAR[r % YS][y]
                straight.append((r * GRID + zl * YS + y, target + zl))
                crossed.append((r * GRID + zl * YS + y, target + 1 - zl))
    first = lax.ppermute(jnp.where(even, upper_rows, lower_rows), PLANE, straight)
    second = lax.ppermute(jnp.where(even, lower_rows, upper_rows), PLANE, crossed)
    solved = ordered(first, second, 2, y_at % 2 == 0)
    kept = jnp.where(even, final0[:SHARD], final0[SHARD:])
    sent = jnp.where(even, final0[SHARD:], final0[:SHARD])
    final0 = ordered(kept, lax.ppermute(sent, "zl", SWAP), 1)
    solution_sub = jnp.concatenate([final0[None], solved[:2]])
    return solution_sub[None, :, None, None], solved[2:, None]


def solution(mesh):
    fine = Mesh(mesh.devices.reshape(2, 4, 4, 2, 8), ("layer",) + PLANE)
    vector = P("layer", None, None, ROW, COL, None)
    vector_top = P(None, ROW, COL, None)
    blocks = P("layer", None, None, ROW, None, COL, None, None)
    pattern = P("layer", None, None, None, ROW, None, COL)
    placed = (vector, vector_top, vector, vector_top, vector, vector_top, blocks, blocks, blocks, blocks, pattern)
    return jax.shard_map(on_device, mesh=fine, in_specs=placed, out_specs=(vector, vector_top), check_vma=False)
```

time: 402 us -> 414 us (1.030)
  the two profiles are of different devices: /device:TPU:6 before, /device:TPU:4 now
where the time goes in v2:
time: 414 us; the launch traced here: 412 us
  starting transfers between devices  163 us (39%)
  waiting for transfers between devices  163 us (39%)
  local copies, waits for them, and re-layouts  33.5 us (8%)
  matrix products  31.3 us (8%)
  blocking collectives  8.1 us (2%)
  between operations  6.6 us (2%)
  other arithmetic  6.14 us (1%)
    all_to_all x7, starting transfers between devices, gather(): lax.all_to_all(jnp.broadcast_to(chunk[None], (size,) + chunk.shape), axes...  76.7 us
    all_to_all x7, waiting for transfers between devices, gather(): lax.all_to_all(jnp.broadcast_to(chunk[None], (size,) + chunk.shape), axes...  62.7 us
    all_to_all x6, waiting for transfers between devices, reduce_row(): lax.all_to_all(partial.reshape(YS, CHUNK, partial.shape[1]), 'y', 0, 0, t...  38.9 us
    all_to_all x6, starting transfers between devices, reduce_row(): lax.all_to_all(partial.reshape(YS, CHUNK, partial.shape[1]), 'y', 0, 0, t...  33.2 us
    ppermute x6, waiting for transfers between devices, turn(): return lax.ppermute(chunk, PLANE, pairs)  29.6 us
    dot_general x33, matrix products, dot(): return jnp.dot(a, b, precision=lax.Precision.HIGH)  27.8 us
    ppermute x6, starting transfers between devices, turn(): return lax.ppermute(chunk, PLANE, pairs)  19.4 us
    ppermute x1, waiting for transfers between devices, on_device(): lax.ppermute(jnp.concatenate([send, lower_inv_sub[0, :1, 0, 0]]), 'zl', S...  18.1 us
  transfers between devices with their start and end apart: 29, of which 21 were waited for; matrix products, arithmetic and copies ran while one was open for 13% of the time, Pallas kernels for 0%

profile of v2, /device:TPU:4, one launch (start us, length us, event | category | flops | bytes accessed | tf_op | source)
XLA Modules:
  0.0 411.5 jit_solution(10774849726343247526)
XLA Ops:
  3.4 9.1 %all-to-all-start = ((f32[16,4,16,256]{3,2,1,0:T(8,128)}), f32[16,4,16,256]{3,2,1,0:T(8,128)S(1)}, u32[]{:S(2)}, u32[]{:S(2)}) async-start(f32[16,4,16,256]{3,2,1,0:T(8,128)} %broadcast_in_dim.113), calls=%async_computation | async-start | bytes 2097152 | tf_op jit(solution)/shard_map/all_to_all | solution.py:45
  14.3 3.8 collective-permute-start.3
  18.9 2.0 collective-permute-start
  22.0 4.0 collective-permute-start.4
  26.8 2.0 collective-permute-start.6
  28.8 18.1 %collective-permute-done = f32[5,16,256]{2,1,0:T(8,128)S(1)} collective-permute-done((f32[5,16,256]{2,1,0:T(8,128)S(1)}, f32[5,16,256]{2,1,0:T(8,128)S(1)}, u32[]{:S(2)}, u32[]{:S(2)}) %collective-permute-start) | collective-permute-done | bytes 81952 | tf_op jit(solution)/shard_map/ppermute | solution.py:96
  49.2 2.7 collective-permute-start.2
  53.1 22.5 %all-to-all-start.1 = ((f32[16,32,512]{2,1,0:T(8,128)}), f32[16,32,512]{2,1,0:T(8,128)S(1)}, u32[]{:S(2)}, u32[]{:S(2)}) async-start(f32[16,32,512]{2,1,0:T(8,128)} %broadcast_in_dim.115), calls=%async_computation.1 | async-start | bytes 2097152 | tf_op jit(solution)/shard_map/all_to_all | solution.py:45
  83.8 1.5 select_select_fusion.1
  87.2 1.5 fusion.20
  88.7 20.9 %all-to-all-done.1 = f32[16,32,512]{2,1,0:T(8,128)S(1)} async-done(((f32[16,32,512]{2,1,0:T(8,128)}), f32[16,32,512]{2,1,0:T(8,128)S(1)}, u32[]{:S(2)}, u32[]{:S(2)}) %all-to-all-start.1) | async-done | bytes 1048608 | tf_op jit(solution)/shard_map/all_to_all | solution.py:45
  112.0 11.4 %all-to-all-start.2 = ((f32[8,32,256]{2,1,0:T(8,128)}), f32[8,32,256]{2,1,0:T(8,128)S(1)}, u32[]{:S(2)}, u32[]{:S(2)}) async-start(f32[8,32,256]{2,1,0:T(8,128)} %bitcast.43), calls=%async_computation.2 | async-start | bytes 524288 | tf_op jit(solution)/shard_map/all_to_all | solution.py:53
  123.4 2.0 slice_bitcast_fusion.17
  126.5 8.4 %all-to-all-done.2 = f32[8,32,256]{2,1,0:T(8,128)S(1)} async-done(((f32[8,32,256]{2,1,0:T(8,128)}), f32[8,32,256]{2,1,0:T(8,128)S(1)}, u32[]{:S(2)}, u32[]{:S(2)}) %all-to-all-start.2) | async-done | bytes 262176 | tf_op jit(solution)/shard_map/all_to_all | solution.py:53
  134.9 1.9 collective-permute-start.5
  136.8 2.0 slice_bitcast_fusion.16
  138.9 5.8 %collective-permute-done.5 = f32[32,256]{1,0:T(8,128)S(1)} collective-permute-done((f32[32,256]{1,0:T(8,128)S(1)}, f32[32,256]{1,0:T(8,128)S(1)}, u32[]{:S(2)}, u32[]{:S(2)}) %collective-permute-start.5) | collective-permute-done | bytes 32800 | tf_op jit(solution)/shard_map/ppermute | solution.py:41
  145.6 6.8 %all-to-all-start.3 = ((f32[16,32,256]{2,1,0:T(8,128)}), f32[16,32,256]{2,1,0:T(8,128)S(1)}, u32[]{:S(2)}, u32[]{:S(2)}) async-start(f32[16,32,256]{2,1,0:T(8,128)} %broadcast_in_dim.126), calls=%async_computation.3 | async-start | bytes 1048576 | tf_op jit(solution)/shard_map/all_to_all | solution.py:45
  154.2 11.1 %all-to-all-done.3 = f32[16,32,256]{2,1,0:T(8,128)S(1)} async-done(((f32[16,32,256]{2,1,0:T(8,128)}), f32[16,32,256]{2,1,0:T(8,128)S(1)}, u32[]{:S(2)}, u32[]{:S(2)}) %all-to-all-start.3) | async-done | bytes 524320 | tf_op jit(solution)/shard_map/all_to_all | solution.py:45
  166.5 3.7 all-to-all-start.4
  170.9 1.3 convolution_select_fusion
  172.5 8.2 %all-to-all-done.4 = f32[8,32,256]{2,1,0:T(8,128)S(1)} async-done(((f32[8,32,256]{2,1,0:T(8,128)}), f32[8,32,256]{2,1,0:T(8,128)S(1)}, u32[]{:S(2)}, u32[]{:S(2)}) %all-to-all-start.4) | async-done | bytes 262176 | tf_op jit(solution)/shard_map/all_to_all | solution.py:53
  180.7 5.5 %collective-permute-start.7 = (f32[32,256]{1,0:T(8,128)S(1)}, f32[32,256]{1,0:T(8,128)S(1)}, u32[]{:S(2)}, u32[]{:S(2)}) collective-permute-start(f32[32,256]{1,0:T(8,128)S(1)} %reduce_sum.64), channel_id=1, source_target_pairs={{0,96},{1,112},{2,48},{3,64},{4,0},{5,16},{6,80},{7,32},{8,104},{9... | collective-permute-start | bytes 98312 | tf_op jit(solution)/shard_map/ppermute | solution.py:41
  186.2 4.3 %collective-permute-done.7 = f32[32,256]{1,0:T(8,128)S(1)} collective-permute-done((f32[32,256]{1,0:T(8,128)S(1)}, f32[32,256]{1,0:T(8,128)S(1)}, u32[]{:S(2)}, u32[]{:S(2)}) %collective-permute-start.7) | collective-permute-done | bytes 32800 | tf_op jit(solution)/shard_map/ppermute | solution.py:41
  191.4 9.7 %all-to-all-start.5 = ((f32[16,32,256]{2,1,0:T(8,128)}), f32[16,32,256]{2,1,0:T(8,128)S(1)}, u32[]{:S(2)}, u32[]{:S(2)}) async-start(f32[16,32,256]{2,1,0:T(8,128)} %broadcast_in_dim.127), calls=%async_computation.5 | async-start | bytes 1048576 | tf_op jit(solution)/shard_map/all_to_all | solution.py:45
  203.1 1.2 fusion.26
  204.8 1.3 convolution_subtract_fusion.9
  206.1 8.0 %all-to-all-done.5 = f32[16,32,256]{2,1,0:T(8,128)S(1)} async-done(((f32[16,32,256]{2,1,0:T(8,128)}), f32[16,32,256]{2,1,0:T(8,128)S(1)}, u32[]{:S(2)}, u32[]{:S(2)}) %all-to-all-start.5) | async-done | bytes 524320 | tf_op jit(solution)/shard_map/all_to_all | solution.py:45
  215.6 3.9 all_to_all.75
  220.3 3.5 all-to-all-start.7
  224.5 2.1 bitcast_multiply_fusion
  226.7 2.9 collective-permute-start.9
  229.6 3.7 all-to-all-done.7
  233.3 3.3 collective-permute-start.8
  236.7 11.6 %collective-permute-done.8 = f32[32,128]{1,0:T(8,128)S(1)} collective-permute-done((f32[32,128]{1,0:T(8,128)S(1)}, f32[32,128]{1,0:T(8,128)S(1)}, u32[]{:S(2)}, u32[]{:S(2)}) %collective-permute-start.8) | collective-permute-done | bytes 16416 | tf_op jit(solution)/shard_map/ppermute | solution.py:41
  249.0 11.3 %all-to-all-start.8 = ((f32[16,32,128]{2,1,0:T(8,128)}), f32[16,32,128]{2,1,0:T(8,128)S(1)}, u32[]{:S(2)}, u32[]{:S(2)}) async-start(f32[16,32,128]{2,1,0:T(8,128)} %broadcast_in_dim.128), calls=%async_computation.8 | async-start | bytes 524288 | tf_op jit(solution)/shard_map/all_to_all | solution.py:45
  260.3 1.9 slice_bitcast_fusion.20
  263.5 6.8 %all-to-all-done.8 = f32[16,32,128]{2,1,0:T(8,128)S(1)} async-done(((f32[16,32,128]{2,1,0:T(8,128)}), f32[16,32,128]{2,1,0:T(8,128)S(1)}, u32[]{:S(2)}, u32[]{:S(2)}) %all-to-all-start.8) | async-done | bytes 262176 | tf_op jit(solution)/shard_map/all_to_all | solution.py:45
  270.5 4.2 %all_to_all.76 = f32[2,512,128]{1,2,0:T(8,128)S(1)} all-to-all(f32[2,512,128]{1,2,0:T(8,128)S(1)} %broadcast_in_dim.130), channel_id=1, replica_groups=mesh['layer'=2,'x'=4,'zh'=4,'zl'=2,'y'=8] {'layer'}, dimensions={0} | all-to-all | bytes 1048576 | tf_op jit(solution)/shard_map/all_to_all | solution.py:45
  276.8 6.7 %all-to-all-start.10 = ((f32[8,32,256]{2,1,0:T(8,128)}), f32[8,32,256]{2,1,0:T(8,128)S(1)}, u32[]{:S(2)}, u32[]{:S(2)}) async-start(f32[8,32,256]{2,1,0:T(8,128)} %bitcast.68), calls=%async_computation.10 | async-start | bytes 524288 | tf_op jit(solution)/shard_map/all_to_all | solution.py:53
  283.5 1.9 slice_bitcast_fusion.9
  285.4 2.0 slice_bitcast_fusion.8
  287.4 8.3 %all-to-all-done.10 = f32[8,32,256]{2,1,0:T(8,128)S(1)} async-done(((f32[8,32,256]{2,1,0:T(8,128)}), f32[8,32,256]{2,1,0:T(8,128)S(1)}, u32[]{:S(2)}, u32[]{:S(2)}) %all-to-all-start.10) | async-done | bytes 262176 | tf_op jit(solution)/shard_map/all_to_all | solution.py:53
  295.7 3.6 collective-permute-start.10
  299.3 2.3 fusion.62
  301.6 3.8 collective-permute-done.10
  306.3 7.8 %all-to-all-start.11 = ((f32[16,32,256]{2,1,0:T(8,128)}), f32[16,32,256]{2,1,0:T(8,128)S(1)}, u32[]{:S(2)}, u32[]{:S(2)}) async-start(f32[16,32,256]{2,1,0:T(8,128)} %broadcast_in_dim.131), calls=%async_computation.11 | async-start | bytes 1048576 | tf_op jit(solution)/shard_map/all_to_all | solution.py:45
  314.1 2.5 fusion.68
  319.8 6.1 %all-to-all-done.11 = f32[16,32,256]{2,1,0:T(8,128)S(1)} async-done(((f32[16,32,256]{2,1,0:T(8,128)}), f32[16,32,256]{2,1,0:T(8,128)S(1)}, u32[]{:S(2)}, u32[]{:S(2)}) %all-to-all-start.11) | async-done | bytes 524320 | tf_op jit(solution)/shard_map/all_to_all | solution.py:45
  325.8 2.1 convolution_subtract_fusion.3
  327.9 4.5 %all-to-all-start.12 = ((f32[8,32,256]{2,1,0:T(8,128)}), f32[8,32,256]{2,1,0:T(8,128)S(1)}, u32[]{:S(2)}, u32[]{:S(2)}) async-start(f32[8,32,256]{2,1,0:T(8,128)} %bitcast.77), calls=%async_computation.12 | async-start | bytes 524288 | tf_op jit(solution)/shard_map/all_to_all | solution.py:53
  332.5 10.3 %all-to-all-done.12 = f32[8,32,256]{2,1,0:T(8,128)S(1)} async-done(((f32[8,32,256]{2,1,0:T(8,128)}), f32[8,32,256]{2,1,0:T(8,128)S(1)}, u32[]{:S(2)}, u32[]{:S(2)}) %all-to-all-start.12) | async-done | bytes 262176 | tf_op jit(solution)/shard_map/all_to_all | solution.py:53
  342.9 4.4 %collective-permute-start.11 = (f32[32,256]{1,0:T(8,128)S(1)}, f32[32,256]{1,0:T(8,128)S(1)}, u32[]{:S(2)}, u32[]{:S(2)}) collective-permute-start(f32[32,256]{1,0:T(8,128)S(1)} %reduce_sum.68), channel_id=1, source_target_pairs={{0,96},{1,112},{2,48},{3,64},{4,0},{5,16},{6,80},{7,32},{8,104},{9... | collective-permute-start | bytes 98312 | tf_op jit(solution)/shard_map/ppermute | solution.py:41
  348.5 4.1 collective-permute-done.11
  353.5 9.5 %all-to-all-start.13 = ((f32[16,32,256]{2,1,0:T(8,128)}), f32[16,32,256]{2,1,0:T(8,128)}, u32[]{:S(2)}, u32[]{:S(2)}) async-start(f32[16,32,256]{2,1,0:T(8,128)} %broadcast_in_dim.132), calls=%async_computation.13 | async-start | bytes 1048576 | tf_op jit(solution)/shard_map/all_to_all | solution.py:45
  363.4 1.9 collective-permute-start.13
  367.2 9.8 %all-to-all-done.13 = f32[16,32,256]{2,1,0:T(8,128)} async-done(((f32[16,32,256]{2,1,0:T(8,128)}), f32[16,32,256]{2,1,0:T(8,128)}, u32[]{:S(2)}, u32[]{:S(2)}) %all-to-all-start.13) | async-done | bytes 524320 | tf_op jit(solution)/shard_map/all_to_all | solution.py:45
  377.0 1.4 fusion.159
  379.5 3.4 all-to-all-start.14
  382.9 10.8 %collective-permute-start.14 = (f32[3,16,256]{2,1,0:T(8,128)S(1)}, f32[3,16,256]{2,1,0:T(8,128)S(1)}, u32[]{:S(2)}, u32[]{:S(2)}) collective-permute-start(f32[3,16,256]{2,1,0:T(8,128)S(1)} %get-tuple-element.42), channel_id=1, source_target_pairs={{0,12},{1,14},{2,6},{3,8},{4,0},{5,2},{6,10},{7,4},{8,13},{9,15},{... | collective-permute-start | bytes 147464 | tf_op jit(solution)/shard_map/ppermute | solution.py:212
  393.8 1.9 collective-permute-start.15
  395.9 9.3 %collective-permute-done.15 = f32[3,16,256]{2,1,0:T(8,128)S(1)} collective-permute-done((f32[3,16,256]{2,1,0:T(8,128)S(1)}, f32[3,16,256]{2,1,0:T(8,128)S(1)}, u32[]{:S(2)}, u32[]{:S(2)}) %collective-permute-start.15) | collective-permute-done | bytes 49184 | tf_op jit(solution)/shard_map/ppermute | solution.py:213
  405.2 1.9 collective-permute-start.12
  407.8 3.1 collective-permute-done.12
  (201 shorter events, 45.5 us)
Async XLA Ops:
  3.4 9.2 %copy-start.27 = (s32[1,4,3,1,1,1,1]{1,6,5,4,3,2,0:T(1,128)S(1)}, s32[1,4,3,1,1,1,1]{1,6,5,4,3,2,0:T(1,128)}, u32[]{:S(2)}) copy-start(s32[1,4,3,1,1,1,1]{1,6,5,4,3,2,0:T(1,128)} %param.22) | copy-start | bytes 148
  3.4 9.9 %copy-start.16 = (f32[1,3,1,1,1,1,256,256]{7,6,5,4,3,2,1,0:T(8,128)S(1)}, f32[1,3,1,1,1,1,256,256]{7,6,5,4,3,2,1,0:T(8,128)}, u32[]{:S(2)}) copy-start(f32[1,3,1,1,1,1,256,256]{7,6,5,4,3,2,1,0:T(8,128)} %param.19) | copy-start | bytes 2359300
  3.4 48.6 %all-to-all-start = ((f32[16,4,16,256]{3,2,1,0:T(8,128)}), f32[16,4,16,256]{3,2,1,0:T(8,128)S(1)}, u32[]{:S(2)}, u32[]{:S(2)}) async-start(f32[16,4,16,256]{3,2,1,0:T(8,128)} %broadcast_in_dim.113), calls=%async_computation | async-start | bytes 2097152 | tf_op jit(solution)/shard_map/all_to_all | solution.py:45
  13.3 4.9 %copy-start.25 = (f32[1,3,1,1,16,512]{5,4,3,2,1,0:T(8,128)S(1)}, f32[1,3,1,1,16,512]{5,4,3,2,1,0:T(8,128)}, u32[]{:S(2)}) copy-start(f32[1,3,1,1,16,512]{5,4,3,2,1,0:T(8,128)} %param.12) | copy-start | bytes 294916
  13.3 4.9 %copy-start.26 = (f32[1,1,16,512]{3,2,1,0:T(8,128)S(1)}, f32[1,1,16,512]{3,2,1,0:T(8,128)}, u32[]{:S(2)}) copy-start(f32[1,1,16,512]{3,2,1,0:T(8,128)} %param.13) | copy-start | bytes 98308
  13.3 7.7 %copy-start.17 = (f32[1,3,1,1,1,1,256,256]{7,6,5,4,3,2,1,0:T(8,128)S(1)}, f32[1,3,1,1,1,1,256,256]{7,6,5,4,3,2,1,0:T(8,128)}, u32[]{:S(2)}) copy-start(f32[1,3,1,1,1,1,256,256]{7,6,5,4,3,2,1,0:T(8,128)} %param.18) | copy-start | bytes 2359300
  14.3 122.5 %collective-permute-start.3 = (f32[3,256,256]{2,1,0:T(8,128)}, f32[3,256,256]{2,1,0:T(8,128)}, u32[]{:S(2)}, u32[]{:S(2)}) collective-permute-start(f32[3,256,256]{2,1,0:T(8,128)} %bitcast_multiply_fusion.2), channel_id=1, source_target_pairs={{0,8},{8,0},{1,9},{9,1},{2,10},{10,2},{3,11},{11,3},{4,12},{12,4},... | collective-permute-start | bytes 2359304 | tf_op jit(solution)/shard_map/ppermute | solution.py:106
  18.9 27.9 %collective-permute-start = (f32[5,16,256]{2,1,0:T(8,128)S(1)}, f32[5,16,256]{2,1,0:T(8,128)S(1)}, u32[]{:S(2)}, u32[]{:S(2)}) collective-permute-start(f32[5,16,256]{2,1,0:T(8,128)S(1)} %pad_maximum_fusion.5), channel_id=1, source_target_pairs={{0,8},{8,0},{1,9},{9,1},{2,10},{10,2},{3,11},{11,3},{4,12},{12,4},... | collective-permute-start | bytes 245768 | tf_op jit(solution)/shard_map/ppermute | solution.py:96
  22.0 27.1 %copy-start.18 = (f32[1,3,1,1,1,1,256,256]{7,6,5,4,3,2,1,0:T(8,128)S(1)}, f32[1,3,1,1,1,1,256,256]{7,6,5,4,3,2,1,0:T(8,128)}, u32[]{:S(2)}) copy-start(f32[1,3,1,1,1,1,256,256]{7,6,5,4,3,2,1,0:T(8,128)} %param.21) | copy-start | bytes 2359300
  22.0 65.2 %collective-permute-start.4 = (f32[1,256,256]{2,1,0:T(8,128)}, f32[1,256,256]{2,1,0:T(8,128)}, u32[]{:S(2)}, u32[]{:S(2)}) collective-permute-start(f32[1,256,256]{2,1,0:T(8,128)} %get-tuple-element.31), channel_id=1, source_target_pairs={{0,8},{8,0},{1,9},{9,1},{2,10},{10,2},{3,11},{11,3},{4,12},{12,4},... | collective-permute-start | bytes 786440 | tf_op jit(solution)/shard_map/ppermute | solution.py:106
  26.8 98.6 %collective-permute-start.6 = (f32[2,256,256]{2,1,0:T(8,128)}, f32[2,256,256]{2,1,0:T(8,128)}, u32[]{:S(2)}, u32[]{:S(2)}) collective-permute-start(f32[2,256,256]{2,1,0:T(8,128)} %slice.297), channel_id=1, source_target_pairs={{0,8},{8,0},{1,9},{9,1},{2,10},{10,2},{3,11},{11,3},{4,12},{12,4},... | collective-permute-start | bytes 1572872 | tf_op jit(solution)/shard_map/ppermute | solution.py:106
  48.4 3.6 collective-permute-start.1
  49.2 211.1 %collective-permute-start.2 = (f32[3,256,256]{2,1,0:T(8,128)S(1)}, f32[3,256,256]{2,1,0:T(8,128)}, u32[]{:S(2)}, u32[]{:S(2)}) collective-permute-start(f32[3,256,256]{2,1,0:T(8,128)S(1)} %bitcast_multiply_fusion.3), channel_id=1, source_target_pairs={{0,8},{8,0},{1,9},{9,1},{2,10},{10,2},{3,11},{11,3},{4,12},{12,4},... | collective-permute-start | bytes 2359304 | tf_op jit(solution)/shard_map/ppermute | solution.py:106
  53.1 56.5 %all-to-all-start.1 = ((f32[16,32,512]{2,1,0:T(8,128)}), f32[16,32,512]{2,1,0:T(8,128)S(1)}, u32[]{:S(2)}, u32[]{:S(2)}) async-start(f32[16,32,512]{2,1,0:T(8,128)} %broadcast_in_dim.115), calls=%async_computation.1 | async-start | bytes 2097152 | tf_op jit(solution)/shard_map/all_to_all | solution.py:45
  81.9 1.8 copy-start.38
  81.9 1.8 copy-start.41
  81.9 1.8 copy-start.34
  82.0 1.8 copy-start.36
  82.0 1.8 copy-start.30
  82.0 1.8 copy-start.32
  83.7 1.6 copy-start.45
  86.1 1.1 copy-start.2
  112.0 22.9 %all-to-all-start.2 = ((f32[8,32,256]{2,1,0:T(8,128)}), f32[8,32,256]{2,1,0:T(8,128)S(1)}, u32[]{:S(2)}, u32[]{:S(2)}) async-start(f32[8,32,256]{2,1,0:T(8,128)} %bitcast.43), calls=%async_computation.2 | async-start | bytes 524288 | tf_op jit(solution)/shard_map/all_to_all | solution.py:53
  134.9 9.8 %collective-permute-start.5 = (f32[32,256]{1,0:T(8,128)S(1)}, f32[32,256]{1,0:T(8,128)S(1)}, u32[]{:S(2)}, u32[]{:S(2)}) collective-permute-start(f32[32,256]{1,0:T(8,128)S(1)} %reduce_sum.63), channel_id=1, source_target_pairs={{0,96},{1,112},{2,48},{3,64},{4,0},{5,16},{6,80},{7,32},{8,104},{9... | collective-permute-start | bytes 98312 | tf_op jit(solution)/shard_map/ppermute | solution.py:41
  145.6 19.8 %all-to-all-start.3 = ((f32[16,32,256]{2,1,0:T(8,128)}), f32[16,32,256]{2,1,0:T(8,128)S(1)}, u32[]{:S(2)}, u32[]{:S(2)}) async-start(f32[16,32,256]{2,1,0:T(8,128)} %broadcast_in_dim.126), calls=%async_computation.3 | async-start | bytes 1048576 | tf_op jit(solution)/shard_map/all_to_all | solution.py:45
  166.5 3.7 copy-start.14
  166.5 3.7 copy-start.33
  166.5 3.8 copy-start.35
  166.5 3.8 copy-start.37
  166.5 3.8 copy-start.42
  166.5 14.2 %all-to-all-start.4 = ((f32[8,32,256]{2,1,0:T(8,128)}), f32[8,32,256]{2,1,0:T(8,128)S(1)}, u32[]{:S(2)}, u32[]{:S(2)}) async-start(f32[8,32,256]{2,1,0:T(8,128)} %bitcast.53), calls=%async_computation.4 | async-start | bytes 524288 | tf_op jit(solution)/shard_map/all_to_all | solution.py:53
  180.7 9.8 %collective-permute-start.7 = (f32[32,256]{1,0:T(8,128)S(1)}, f32[32,256]{1,0:T(8,128)S(1)}, u32[]{:S(2)}, u32[]{:S(2)}) collective-permute-start(f32[32,256]{1,0:T(8,128)S(1)} %reduce_sum.64), channel_id=1, source_target_pairs={{0,96},{1,112},{2,48},{3,64},{4,0},{5,16},{6,80},{7,32},{8,104},{9... | collective-permute-start | bytes 98312 | tf_op jit(solution)/shard_map/ppermute | solution.py:41
  191.4 10.1 %copy-start.11 = (f32[256,256]{1,0:T(8,128)S(1)}, f32[256,256]{1,0:T(8,128)}, u32[]{:S(2)}) copy-start(f32[256,256]{1,0:T(8,128)} %get-tuple-element.27) | copy-start | bytes 786436
  191.4 22.7 %all-to-all-start.5 = ((f32[16,32,256]{2,1,0:T(8,128)}), f32[16,32,256]{2,1,0:T(8,128)S(1)}, u32[]{:S(2)}, u32[]{:S(2)}) async-start(f32[16,32,256]{2,1,0:T(8,128)} %broadcast_in_dim.127), calls=%async_computation.5 | async-start | bytes 1048576 | tf_op jit(solution)/shard_map/all_to_all | solution.py:45
  202.1 1.0 copy-start.10
  203.1 1.2 copy-start.4
  203.1 1.2 copy-start.9
  204.8 9.3 %copy-start.1 = (f32[256,512]{1,0:T(8,128)S(1)}, f32[256,512]{1,0:T(8,128)}, u32[]{:S(2)}) copy-start(f32[256,512]{1,0:T(8,128)} %fusion.26) | copy-start | bytes 1572868
  220.3 12.9 %all-to-all-start.7 = ((f32[8,32,128]{2,1,0:T(8,128)}), f32[8,32,128]{2,1,0:T(8,128)S(1)}, u32[]{:S(2)}, u32[]{:S(2)}) async-start(f32[8,32,128]{2,1,0:T(8,128)} %bitcast.57), calls=%async_computation.7 | async-start | bytes 262144 | tf_op jit(solution)/shard_map/all_to_all | solution.py:53
  226.7 58.7 %collective-permute-start.9 = (f32[3,256,256]{2,1,0:T(8,128)}, f32[3,256,256]{2,1,0:T(8,128)}, u32[]{:S(2)}, u32[]{:S(2)}) collective-permute-start(f32[3,256,256]{2,1,0:T(8,128)} %bitcast_multiply_fusion), channel_id=1, source_target_pairs={{0,8},{8,0},{1,9},{9,1},{2,10},{10,2},{3,11},{11,3},{4,12},{12,4},... | collective-permute-start | bytes 2359304 | tf_op jit(solution)/shard_map/ppermute | solution.py:106
  233.3 15.0 %collective-permute-start.8 = (f32[32,128]{1,0:T(8,128)S(1)}, f32[32,128]{1,0:T(8,128)S(1)}, u32[]{:S(2)}, u32[]{:S(2)}) collective-permute-start(f32[32,128]{1,0:T(8,128)S(1)} %reduce_sum.66), channel_id=1, source_target_pairs={{0,96},{1,112},{2,48},{3,64},{4,0},{5,16},{6,80},{7,32},{8,104},{9... | collective-permute-start | bytes 49160 | tf_op jit(solution)/shard_map/ppermute | solution.py:41
  249.0 21.3 %all-to-all-start.8 = ((f32[16,32,128]{2,1,0:T(8,128)}), f32[16,32,128]{2,1,0:T(8,128)S(1)}, u32[]{:S(2)}, u32[]{:S(2)}) async-start(f32[16,32,128]{2,1,0:T(8,128)} %broadcast_in_dim.128), calls=%async_computation.8 | async-start | bytes 524288 | tf_op jit(solution)/shard_map/all_to_all | solution.py:45
  260.3 1.9 copy-start.46
  276.8 18.9 %all-to-all-start.10 = ((f32[8,32,256]{2,1,0:T(8,128)}), f32[8,32,256]{2,1,0:T(8,128)S(1)}, u32[]{:S(2)}, u32[]{:S(2)}) async-start(f32[8,32,256]{2,1,0:T(8,128)} %bitcast.68), calls=%async_computation.10 | async-start | bytes 524288 | tf_op jit(solution)/shard_map/all_to_all | solution.py:53
  287.4 11.9 %copy-start.23 = (f32[256,256]{1,0:T(8,128)S(1)}, f32[256,256]{1,0:T(8,128)}, u32[]{:S(2)}) copy-start(f32[256,256]{1,0:T(8,128)} %get-tuple-element.20) | copy-start | bytes 786436
  295.7 9.7 %collective-permute-start.10 = (f32[32,256]{1,0:T(8,128)S(1)}, f32[32,256]{1,0:T(8,128)S(1)}, u32[]{:S(2)}, u32[]{:S(2)}) collective-permute-start(f32[32,256]{1,0:T(8,128)S(1)} %reduce_sum.67), channel_id=1, source_target_pairs={{0,96},{1,112},{2,48},{3,64},{4,0},{5,16},{6,80},{7,32},{8,104},{9... | collective-permute-start | bytes 98312 | tf_op jit(solution)/shard_map/ppermute | solution.py:41
  306.3 7.8 %copy-start.24 = (f32[256,256]{1,0:T(8,128)S(1)}, f32[256,256]{1,0:T(8,128)}, u32[]{:S(2)}) copy-start(f32[256,256]{1,0:T(8,128)} %get-tuple-element.11) | copy-start | bytes 786436
  306.3 19.6 %all-to-all-start.11 = ((f32[16,32,256]{2,1,0:T(8,128)}), f32[16,32,256]{2,1,0:T(8,128)S(1)}, u32[]{:S(2)}, u32[]{:S(2)}) async-start(f32[16,32,256]{2,1,0:T(8,128)} %broadcast_in_dim.131), calls=%async_computation.11 | async-start | bytes 1048576 | tf_op jit(solution)/shard_map/all_to_all | solution.py:45
  316.6 1.0 copy-start.20
  318.6 7.3 %copy-start.19 = (f32[256,512]{1,0:T(8,128)S(1)}, f32[256,512]{1,0:T(8,128)}, u32[]{:S(2)}) copy-start(f32[256,512]{1,0:T(8,128)} %fusion.68) | copy-start | bytes 1572868
  327.9 4.5 %copy-start.15 = (f32[16,1,16,256]{3,2,1,0:T(8,128)S(1)}, f32[16,1,16,256]{3,2,1,0:T(8,128)}, u32[]{:S(2)}) copy-start(f32[16,1,16,256]{3,2,1,0:T(8,128)} %get-tuple-element.6) | copy-start | bytes 786436
  327.9 15.0 %all-to-all-start.12 = ((f32[8,32,256]{2,1,0:T(8,128)}), f32[8,32,256]{2,1,0:T(8,128)S(1)}, u32[]{:S(2)}, u32[]{:S(2)}) async-start(f32[8,32,256]{2,1,0:T(8,128)} %bitcast.77), calls=%async_computation.12 | async-start | bytes 524288 | tf_op jit(solution)/shard_map/all_to_all | solution.py:53
  342.9 9.7 %collective-permute-start.11 = (f32[32,256]{1,0:T(8,128)S(1)}, f32[32,256]{1,0:T(8,128)S(1)}, u32[]{:S(2)}, u32[]{:S(2)}) collective-permute-start(f32[32,256]{1,0:T(8,128)S(1)} %reduce_sum.68), channel_id=1, source_target_pairs={{0,96},{1,112},{2,48},{3,64},{4,0},{5,16},{6,80},{7,32},{8,104},{9... | collective-permute-start | bytes 98312 | tf_op jit(solution)/shard_map/ppermute | solution.py:41
  353.5 9.5 %copy-start.8 = (f32[256,256]{1,0:T(8,128)S(1)}, f32[256,256]{1,0:T(8,128)}, u32[]{:S(2)}) copy-start(f32[256,256]{1,0:T(8,128)} %get-tuple-element.15) | copy-start | bytes 786436
  353.5 23.5 %all-to-all-start.13 = ((f32[16,32,256]{2,1,0:T(8,128)}), f32[16,32,256]{2,1,0:T(8,128)}, u32[]{:S(2)}, u32[]{:S(2)}) async-start(f32[16,32,256]{2,1,0:T(8,128)} %broadcast_in_dim.132), calls=%async_computation.13 | async-start | bytes 1048576 | tf_op jit(solution)/shard_map/all_to_all | solution.py:45
  363.0 2.4 copy-start.7
  363.4 3.1 collective-permute-start.13
  365.3 1.1 copy-start
  379.5 25.7 %all-to-all-start.14 = ((f32[8,32,256]{2,1,0:T(8,128)}), f32[8,32,256]{2,1,0:T(8,128)S(1)}, u32[]{:S(2)}, u32[]{:S(2)}) async-start(f32[8,32,256]{2,1,0:T(8,128)} %bitcast.79), calls=%async_computation.14 | async-start | bytes 524288 | tf_op jit(solution)/shard_map/all_to_all | solution.py:53
  382.9 12.9 %collective-permute-start.14 = (f32[3,16,256]{2,1,0:T(8,128)S(1)}, f32[3,16,256]{2,1,0:T(8,128)S(1)}, u32[]{:S(2)}, u32[]{:S(2)}) collective-permute-start(f32[3,16,256]{2,1,0:T(8,128)S(1)} %get-tuple-element.42), channel_id=1, source_target_pairs={{0,12},{1,14},{2,6},{3,8},{4,0},{5,2},{6,10},{7,4},{8,13},{9,15},{... | collective-permute-start | bytes 147464 | tf_op jit(solution)/shard_map/ppermute | solution.py:212
  393.8 11.4 %collective-permute-start.15 = (f32[3,16,256]{2,1,0:T(8,128)S(1)}, f32[3,16,256]{2,1,0:T(8,128)S(1)}, u32[]{:S(2)}, u32[]{:S(2)}) collective-permute-start(f32[3,16,256]{2,1,0:T(8,128)S(1)} %get-tuple-element.43), channel_id=1, source_target_pairs={{0,13},{1,15},{2,7},{3,9},{4,1},{5,3},{6,11},{7,5},{8,12},{9,14},{... | collective-permute-start | bytes 147464 | tf_op jit(solution)/shard_map/ppermute | solution.py:213
  405.2 2.6 copy-start.21
  405.2 5.6 %collective-permute-start.12 = (f32[16,256]{1,0:T(8,128)S(1)}, f32[16,256]{1,0:T(8,128)S(1)}, u32[]{:S(2)}, u32[]{:S(2)}) collective-permute-start(f32[16,256]{1,0:T(8,128)S(1)} %get-tuple-element.47), channel_id=1, source_target_pairs={{0,8},{8,0},{1,9},{9,1},{2,10},{10,2},{3,11},{11,3},{4,12},{12,4},... | collective-permute-start | bytes 49160 | tf_op jit(solution)/shard_map/ppermute | solution.py:217
  407.8 3.1 slice-start
  (15 other events, 11.9 us)

commit v3 on v2

--- a/solution.py
+++ b/solution.py
@@ -88,7 +88,11 @@
     upper_inv = jnp.concatenate([upper_inv_sub[0, :, 0, 0], upper_inv_top[:, 0]])
     row_at = lax.broadcasted_iota(jnp.int32, (4, SHARD, W), 1) + col * SHARD
     col_at = lax.broadcasted_iota(jnp.int32, (4, SHARD, W), 2)
-    packed = gather(jnp.where(col_at < row_at, lower_inv, upper_inv), COL, GRID)
+    packed = gather(jnp.where(col_at < row_at, lower_inv, upper_inv), "y", YS)
+    packed = packed.transpose(1, 0, 2, 3).reshape(4, W // 2, W)
+    packed1 = lax.ppermute(packed[1], "zl", SWAP)
+    packed2 = lax.ppermute(jnp.concatenate([packed[:1], packed[2:]]), "zl", SWAP)
+    whole1 = ordered(packed[1], packed1, 0)
 
     rhs = jnp.concatenate([rhs_sub[0, :, 0, 0], rhs_top[:, 0]])
     keep = jnp.where(even, rhs[:, :, :HALF], rhs[:, :, HALF:])
@@ -112,7 +116,6 @@
     up_top = both(masked(upper_top, 3))
     up_sub = both(masked(upper_sub, 2))
 
-    packed = packed.reshape(GRID, 4, SHARD, W)
     natural = lax.broadcasted_iota(jnp.int32, (W, W), 0)
     across = lax.broadcasted_iota(jnp.int32, (W, W), 1)
     table = jnp.array(NEAR, jnp.int32)
@@ -122,8 +125,7 @@
     for y in range(YS):
         moved = moved + jnp.where(slot == y, mine[y] * CHUNK, 0)
     pick = (across == moved).astype(jnp.float32)
-    whole = [packed[:, k].reshape(W, W) for k in range(4)]
-    near = [None] + [jnp.dot(pick, whole[k], precision=lax.Precision.HIGHEST) for k in (1, 2, 3)]
+    near1 = jnp.dot(pick, whole1, precision=lax.Precision.HIGHEST)
 
     def lower_of(matrix, down):
         return jnp.where(across < down, matrix, jnp.where(across == down, 1.0, 0.0))
@@ -131,13 +133,8 @@
     def upper_of(matrix, down):
         return jnp.where(across >= down, matrix, 0.0)
 
-    lower1 = lower_of(near[1], moved)
-    lower2 = lower_of(near[2], moved)
-    top = dot(upper_of(near[3], moved), lower_of(whole[3], natural))
-    upper2 = upper_of(near[2], moved)
-    upper1 = upper_of(near[1], moved)
-    upper0 = upper_of(whole[0], natural)
-    upper0 = upper0.reshape(2, YS, SHARD, W).transpose(1, 0, 2, 3).reshape(W, W)
+    lower1 = lower_of(near1, moved)
+    upper1 = upper_of(near1, moved)
 
     def columns(matrix):
         left = lax.dynamic_slice(matrix, (0, y_at * SHARD), (W, SHARD))
@@ -146,22 +143,30 @@
 
     low10 = dot(lower1, low_sub[0])
     share1 = dot(columns(lower1), rhs[1])
+
+    def own(pair):
+        return jnp.where(row < YS, pair[:W], pair[W:])
+
+    start = start.reshape(2, YS, 2, SHARD, W + HALF).transpose(0, 2, 1, 3, 4).reshape(2, W, W + HALF)
+    y0 = jnp.concatenate([dot(start[s, :, :W], start[s, :, W:]) for s in range(2)])
+
+    y1 = reduce_row(share1 - dot(low10, y0))
+    packed2 = lax.optimization_barrier((packed2, y1))[0]
+    y1 = turn(y1, NEAR)
+    whole0, whole2, whole3 = [ordered(packed[k], packed2[j], 0) for j, k in enumerate((0, 2, 3))]
+    near2 = jnp.dot(pick, whole2, precision=lax.Precision.HIGHEST)
+    near3 = jnp.dot(pick, whole3, precision=lax.Precision.HIGHEST)
+    lower2 = lower_of(near2, moved)
+    top = dot(upper_of(near3, moved), lower_of(whole3, natural))
+    upper2 = upper_of(near2, moved)
+    upper0 = upper_of(whole0, natural)
+    upper0 = upper0.reshape(2, YS, SHARD, W).transpose(1, 0, 2, 3).reshape(W, W)
     share2 = dot(columns(lower2), rhs[2])
     share3 = dot(columns(top), rhs[3]) * (layer == 0).astype(jnp.float32)
-
     own_column = (row % YS == y_at).astype(jnp.float32)
     diag2 = upper2 * own_column
     diag1 = upper1 * own_column
     diag0 = upper0 * own_column
-
-    def own(pair):
-        return jnp.where(row < YS, pair[:W], pair[W:])
-
-    start = start.reshape(2, YS, 2, SHARD, W + HALF).transpose(0, 2, 1, 3, 4).reshape(2, W, W + HALF)
-    y0 = jnp.concatenate([dot(start[s, :, :W], start[s, :, W:]) for s in range(2)])
-
-    y1 = reduce_row(share1 - dot(low10, y0))
-    y1 = turn(y1, NEAR)
     low20 = dot(lower2, low_sub[1])
     low21 = dot(lower2, low_sub[2])
     share2 = share2 - dot(low20, y0)

time: 414 us -> 413 us (level)
  waiting for transfers between devices: 163 us -> 136 us
  starting transfers between devices: 163 us -> 175 us
  local copies, waits for them, and re-layouts: 33.5 us -> 43.8 us
    all_to_all x7, waiting for transfers between devices: 62.7 us -> 38.2 us  [gather(): lax.all_to_all(jnp.broadcast_to(chunk[None], (size,) + chunk.shape), axes...]
    ppermute x0 -> x2, waiting for transfers between devices: none -> 23.5 us  [the longest x1 23.5 us: on_device(): packed1 = lax.ppermute(packed[1], 'zl', SWAP)]
    ppermute x1, waiting for transfers between devices: 18.1 us -> 0.01 us  [on_device(): lax.ppermute(jnp.concatenate([send, lower_inv_sub[0, :1, 0, 0]]), 'zl', S...]
    ppermute x6, starting transfers between devices: 19.4 us -> 29.7 us  [turn(): return lax.ppermute(chunk, PLANE, pairs)]
    ppermute x0 -> x2, starting transfers between devices: none -> 9.87 us  [the longest x1 6.62 us: on_device(): packed1 = lax.ppermute(packed[1], 'zl', SWAP)]
    all_to_all x6, starting transfers between devices: 33.2 us -> 25.4 us  [reduce_row(): lax.all_to_all(partial.reshape(YS, CHUNK, partial.shape[1]), 'y', 0, 0, t...]
    ppermute x6, waiting for transfers between devices: 29.6 us -> 23.8 us  [turn(): return lax.ppermute(chunk, PLANE, pairs)]
    squeeze x0 -> x5, local copies, waits for them, and re-layouts: none -> 4.36 us  [the longest x1 1.77 us: on_device(): packed2[j]]
  transfers between devices with their start and end apart: 29 -> 31, of which waited for: 21 -> 18; matrix products, arithmetic and copies ran while one was open for 13% -> 15% of each run, Pallas kernels for 0% -> 0%
where the time goes in v3:
time: 413 us; the launch traced here: 409 us
  starting transfers between devices  175 us (42%)
  waiting for transfers between devices  136 us (33%)
  local copies, waits for them, and re-layouts  43.8 us (11%)
  matrix products  31.7 us (8%)
  blocking collectives  8.23 us (2%)
  other arithmetic  7.38 us (2%)
  between operations  6.88 us (2%)
    all_to_all x7, starting transfers between devices, gather(): lax.all_to_all(jnp.broadcast_to(chunk[None], (size,) + chunk.shape), axes...  75.6 us
    all_to_all x6, waiting for transfers between devices, reduce_row(): lax.all_to_all(partial.reshape(YS, CHUNK, partial.shape[1]), 'y', 0, 0, t...  38.3 us
    all_to_all x7, waiting for transfers between devices, gather(): lax.all_to_all(jnp.broadcast_to(chunk[None], (size,) + chunk.shape), axes...  38.2 us
    ppermute x6, starting transfers between devices, turn(): return lax.ppermute(chunk, PLANE, pairs)  29.7 us
    dot_general x33, matrix products, dot(): return jnp.dot(a, b, precision=lax.Precision.HIGH)  28.4 us
    all_to_all x6, starting transfers between devices, reduce_row(): lax.all_to_all(partial.reshape(YS, CHUNK, partial.shape[1]), 'y', 0, 0, t...  25.4 us
    ppermute x6, waiting for transfers between devices, turn(): return lax.ppermute(chunk, PLANE, pairs)  23.8 us
    ppermute x1, waiting for transfers between devices, on_device(): packed1 = lax.ppermute(packed[1], 'zl', SWAP)  23.5 us
  transfers between devices with their start and end apart: 31, of which 18 were waited for; matrix products, arithmetic and copies ran while one was open for 15% of the time, Pallas kernels for 0%

profile of v3, /device:TPU:4, one launch (start us, length us, event | category | flops | bytes accessed | tf_op | source)
XLA Modules:
  0.0 409.3 jit_solution(7999074343707876560)
XLA Ops:
  3.1 7.2 %all-to-all-start = ((f32[8,4,16,256]{3,2,1,0:T(8,128)}), f32[8,4,16,256]{3,2,1,0:T(8,128)S(1)}, u32[]{:S(2)}, u32[]{:S(2)}) async-start(f32[8,4,16,256]{3,2,1,0:T(8,128)} %broadcast_in_dim.113), calls=%async_computation | async-start | bytes 1048576 | tf_op jit(solution)/shard_map/all_to_all | solution.py:45
  11.7 4.4 %collective-permute-start.3 = (f32[1,256,256]{2,1,0:T(8,128)}, f32[1,256,256]{2,1,0:T(8,128)}, u32[]{:S(2)}, u32[]{:S(2)}) collective-permute-start(f32[1,256,256]{2,1,0:T(8,128)} %get-tuple-element.29), channel_id=1, source_target_pairs={{0,8},{8,0},{1,9},{9,1},{2,10},{10,2},{3,11},{11,3},{4,12},{12,4},... | collective-permute-start | bytes 786440 | tf_op jit(solution)/shard_map/ppermute | solution.py:110
  16.8 1.9 collective-permute-start.2
  18.9 4.1 collective-permute-start.6
  23.8 1.9 collective-permute-start.8
  28.1 3.9 collective-permute-start.5
  33.2 21.9 %all-to-all-start.1 = ((f32[16,32,512]{2,1,0:T(8,128)}), f32[16,32,512]{2,1,0:T(8,128)S(1)}, u32[]{:S(2)}, u32[]{:S(2)}) async-start(f32[16,32,512]{2,1,0:T(8,128)} %broadcast_in_dim.124), calls=%async_computation.1 | async-start | bytes 2097152 | tf_op jit(solution)/shard_map/all_to_all | solution.py:45
  59.3 1.6 copy.70
  60.9 6.6 %collective-permute-start.1 = (f32[128,256]{0,1:T(8,128)}, f32[128,256]{0,1:T(8,128)}, u32[]{:S(2)}, u32[]{:S(2)}) collective-permute-start(f32[128,256]{0,1:T(8,128)} %copy.70), channel_id=1, source_target_pairs={{0,8},{8,0},{1,9},{9,1},{2,10},{10,2},{3,11},{11,3},{4,12},{12,4},... | collective-permute-start | bytes 393224 | tf_op jit(solution)/shard_map/ppermute | solution.py:93
  74.8 1.8 pad_maximum_fusion.1
  76.5 23.5 %collective-permute-done.1 = f32[128,256]{0,1:T(8,128)} collective-permute-done((f32[128,256]{0,1:T(8,128)}, f32[128,256]{0,1:T(8,128)}, u32[]{:S(2)}, u32[]{:S(2)}) %collective-permute-start.1) | collective-permute-done | bytes 131104 | tf_op jit(solution)/shard_map/ppermute | solution.py:93
  100.0 3.3 collective-permute-start
  103.9 2.0 select_select_fusion.1
  105.9 1.8 fusion.129
  107.8 2.3 fusion.2
  112.6 3.8 all-to-all-start.2
  116.4 1.8 slice_bitcast_fusion.10
  118.2 2.0 slice_bitcast_fusion.16
  121.3 5.6 %all-to-all-done.2 = f32[8,32,256]{2,1,0:T(8,128)S(1)} async-done(((f32[8,32,256]{2,1,0:T(8,128)}), f32[8,32,256]{2,1,0:T(8,128)S(1)}, u32[]{:S(2)}, u32[]{:S(2)}) %all-to-all-start.2) | async-done | bytes 262176 | tf_op jit(solution)/shard_map/all_to_all | solution.py:53
  126.9 13.4 %collective-permute-start.7 = (f32[32,256]{1,0:T(8,128)S(1)}, f32[32,256]{1,0:T(8,128)S(1)}, u32[]{:S(2)}, u32[]{:S(2)}) collective-permute-start(f32[32,256]{1,0:T(8,128)S(1)} %reduce_sum.63), channel_id=1, source_target_pairs={{0,96},{1,112},{2,48},{3,64},{4,0},{5,16},{6,80},{7,32},{8,104},{9... | collective-permute-start | bytes 98312 | tf_op jit(solution)/shard_map/ppermute | solution.py:41
  140.4 1.8 slice_bitcast_fusion.32
  144.7 8.9 %all-to-all-start.3 = ((f32[16,32,256]{2,1,0:T(8,128)}), f32[16,32,256]{2,1,0:T(8,128)S(1)}, u32[]{:S(2)}, u32[]{:S(2)}) async-start(f32[16,32,256]{2,1,0:T(8,128)} %broadcast_in_dim.126), calls=%async_computation.3 | async-start | bytes 1048576 | tf_op jit(solution)/shard_map/all_to_all | solution.py:45
  154.8 1.4 fusion.38
  157.0 9.2 %all-to-all-done.3 = f32[16,32,256]{2,1,0:T(8,128)S(1)} async-done(((f32[16,32,256]{2,1,0:T(8,128)}), f32[16,32,256]{2,1,0:T(8,128)S(1)}, u32[]{:S(2)}, u32[]{:S(2)}) %all-to-all-start.3) | async-done | bytes 524320 | tf_op jit(solution)/shard_map/all_to_all | solution.py:45
  167.3 3.5 all-to-all-start.4
  172.2 9.1 %all-to-all-done.4 = f32[8,32,256]{2,1,0:T(8,128)S(1)} async-done(((f32[8,32,256]{2,1,0:T(8,128)}), f32[8,32,256]{2,1,0:T(8,128)S(1)}, u32[]{:S(2)}, u32[]{:S(2)}) %all-to-all-start.4) | async-done | bytes 262176 | tf_op jit(solution)/shard_map/all_to_all | solution.py:53
  181.3 4.7 %collective-permute-start.9 = (f32[32,256]{1,0:T(8,128)S(1)}, f32[32,256]{1,0:T(8,128)S(1)}, u32[]{:S(2)}, u32[]{:S(2)}) collective-permute-start(f32[32,256]{1,0:T(8,128)S(1)} %reduce_sum.64), channel_id=1, source_target_pairs={{0,96},{1,112},{2,48},{3,64},{4,0},{5,16},{6,80},{7,32},{8,104},{9... | collective-permute-start | bytes 98312 | tf_op jit(solution)/shard_map/ppermute | solution.py:41
  186.0 5.0 %collective-permute-done.9 = f32[32,256]{1,0:T(8,128)S(1)} collective-permute-done((f32[32,256]{1,0:T(8,128)S(1)}, f32[32,256]{1,0:T(8,128)S(1)}, u32[]{:S(2)}, u32[]{:S(2)}) %collective-permute-start.9) | collective-permute-done | bytes 32800 | tf_op jit(solution)/shard_map/ppermute | solution.py:41
  191.9 9.0 %all-to-all-start.5 = ((f32[16,32,256]{2,1,0:T(8,128)}), f32[16,32,256]{2,1,0:T(8,128)S(1)}, u32[]{:S(2)}, u32[]{:S(2)}) async-start(f32[16,32,256]{2,1,0:T(8,128)} %broadcast_in_dim.127), calls=%async_computation.5 | async-start | bytes 1048576 | tf_op jit(solution)/shard_map/all_to_all | solution.py:45
  205.3 7.7 %all-to-all-done.5 = f32[16,32,256]{2,1,0:T(8,128)S(1)} async-done(((f32[16,32,256]{2,1,0:T(8,128)}), f32[16,32,256]{2,1,0:T(8,128)S(1)}, u32[]{:S(2)}, u32[]{:S(2)}) %all-to-all-start.5) | async-done | bytes 524320 | tf_op jit(solution)/shard_map/all_to_all | solution.py:45
  213.0 1.6 fusion.172
  215.2 3.9 all_to_all.75
  219.9 3.5 all-to-all-start.7
  224.8 3.1 collective-permute-start.11
  227.8 5.1 %all-to-all-done.7 = f32[8,32,128]{2,1,0:T(8,128)S(1)} async-done(((f32[8,32,128]{2,1,0:T(8,128)}), f32[8,32,128]{2,1,0:T(8,128)S(1)}, u32[]{:S(2)}, u32[]{:S(2)}) %all-to-all-start.7) | async-done | bytes 131104 | tf_op jit(solution)/shard_map/all_to_all | solution.py:53
  232.9 3.1 collective-permute-start.10
  236.9 9.5 %collective-permute-done.10 = f32[32,128]{1,0:T(8,128)} collective-permute-done((f32[32,128]{1,0:T(8,128)S(1)}, f32[32,128]{1,0:T(8,128)}, u32[]{:S(2)}, u32[]{:S(2)}) %collective-permute-start.10) | collective-permute-done | bytes 16416 | tf_op jit(solution)/shard_map/ppermute | solution.py:41
  246.3 1.4 broadcast_in_dim.128
  247.8 11.4 %all-to-all-start.8 = ((f32[16,32,128]{2,1,0:T(8,128)}), f32[16,32,128]{2,1,0:T(8,128)}, u32[]{:S(2)}, u32[]{:S(2)}) async-start(f32[16,32,128]{2,1,0:T(8,128)} %broadcast_in_dim.128), calls=%async_computation.8 | async-start | bytes 524288 | tf_op jit(solution)/shard_map/all_to_all | solution.py:45
  259.2 2.0 slice_bitcast_fusion.20
  263.9 5.3 %all-to-all-done.8 = f32[16,32,128]{2,1,0:T(8,128)} async-done(((f32[16,32,128]{2,1,0:T(8,128)}), f32[16,32,128]{2,1,0:T(8,128)}, u32[]{:S(2)}, u32[]{:S(2)}) %all-to-all-start.8) | async-done | bytes 262176 | tf_op jit(solution)/shard_map/all_to_all | solution.py:45
  270.3 4.3 %all_to_all.76 = f32[2,512,128]{1,2,0:T(8,128)S(1)} all-to-all(f32[2,512,128]{1,2,0:T(8,128)S(1)} %broadcast_in_dim.130), channel_id=1, replica_groups=mesh['layer'=2,'x'=4,'zh'=4,'zl'=2,'y'=8] {'layer'}, dimensions={0} | all-to-all | bytes 1048576 | tf_op jit(solution)/shard_map/all_to_all | solution.py:45
  276.9 6.7 %all-to-all-start.10 = ((f32[8,32,256]{2,1,0:T(8,128)}), f32[8,32,256]{2,1,0:T(8,128)S(1)}, u32[]{:S(2)}, u32[]{:S(2)}) async-start(f32[8,32,256]{2,1,0:T(8,128)} %bitcast.75), calls=%async_computation.10 | async-start | bytes 524288 | tf_op jit(solution)/shard_map/all_to_all | solution.py:53
  284.5 2.0 slice_bitcast_fusion.8
  286.5 9.2 %all-to-all-done.10 = f32[8,32,256]{2,1,0:T(8,128)S(1)} async-done(((f32[8,32,256]{2,1,0:T(8,128)}), f32[8,32,256]{2,1,0:T(8,128)S(1)}, u32[]{:S(2)}, u32[]{:S(2)}) %all-to-all-start.10) | async-done | bytes 262176 | tf_op jit(solution)/shard_map/all_to_all | solution.py:53
  295.8 3.6 collective-permute-start.12
  301.3 4.2 %collective-permute-done.12 = f32[32,256]{1,0:T(8,128)S(1)} collective-permute-done((f32[32,256]{1,0:T(8,128)S(1)}, f32[32,256]{1,0:T(8,128)S(1)}, u32[]{:S(2)}, u32[]{:S(2)}) %collective-permute-start.12) | collective-permute-done | bytes 32800 | tf_op jit(solution)/shard_map/ppermute | solution.py:41
  306.4 7.8 %all-to-all-start.11 = ((f32[16,32,256]{2,1,0:T(8,128)}), f32[16,32,256]{2,1,0:T(8,128)S(1)}, u32[]{:S(2)}, u32[]{:S(2)}) async-start(f32[16,32,256]{2,1,0:T(8,128)} %broadcast_in_dim.131), calls=%async_computation.11 | async-start | bytes 1048576 | tf_op jit(solution)/shard_map/all_to_all | solution.py:45
  314.9 1.4 fusion.68
  318.9 7.1 %all-to-all-done.11 = f32[16,32,256]{2,1,0:T(8,128)S(1)} async-done(((f32[16,32,256]{2,1,0:T(8,128)}), f32[16,32,256]{2,1,0:T(8,128)S(1)}, u32[]{:S(2)}, u32[]{:S(2)}) %all-to-all-start.11) | async-done | bytes 524320 | tf_op jit(solution)/shard_map/all_to_all | solution.py:45
  327.1 4.4 %all-to-all-start.12 = ((f32[8,32,256]{2,1,0:T(8,128)}), f32[8,32,256]{2,1,0:T(8,128)S(1)}, u32[]{:S(2)}, u32[]{:S(2)}) async-start(f32[8,32,256]{2,1,0:T(8,128)} %bitcast.84), calls=%async_computation.12 | async-start | bytes 524288 | tf_op jit(solution)/shard_map/all_to_all | solution.py:53
  332.7 9.3 %all-to-all-done.12 = f32[8,32,256]{2,1,0:T(8,128)S(1)} async-done(((f32[8,32,256]{2,1,0:T(8,128)}), f32[8,32,256]{2,1,0:T(8,128)S(1)}, u32[]{:S(2)}, u32[]{:S(2)}) %all-to-all-start.12) | async-done | bytes 262176 | tf_op jit(solution)/shard_map/all_to_all | solution.py:53
  342.0 4.2 %collective-permute-start.13 = (f32[32,256]{1,0:T(8,128)S(1)}, f32[32,256]{1,0:T(8,128)S(1)}, u32[]{:S(2)}, u32[]{:S(2)}) collective-permute-start(f32[32,256]{1,0:T(8,128)S(1)} %reduce_sum.68), channel_id=1, source_target_pairs={{0,96},{1,112},{2,48},{3,64},{4,0},{5,16},{6,80},{7,32},{8,104},{9... | collective-permute-start | bytes 98312 | tf_op jit(solution)/shard_map/ppermute | solution.py:41
  346.6 5.2 %collective-permute-done.13 = f32[32,256]{1,0:T(8,128)S(1)} collective-permute-done((f32[32,256]{1,0:T(8,128)S(1)}, f32[32,256]{1,0:T(8,128)S(1)}, u32[]{:S(2)}, u32[]{:S(2)}) %collective-permute-start.13) | collective-permute-done | bytes 32800 | tf_op jit(solution)/shard_map/ppermute | solution.py:41
  352.6 9.4 %all-to-all-start.13 = ((f32[16,32,256]{2,1,0:T(8,128)}), f32[16,32,256]{2,1,0:T(8,128)}, u32[]{:S(2)}, u32[]{:S(2)}) async-start(f32[16,32,256]{2,1,0:T(8,128)} %broadcast_in_dim.132), calls=%async_computation.13 | async-start | bytes 1048576 | tf_op jit(solution)/shard_map/all_to_all | solution.py:45
  362.5 1.9 collective-permute-start.15
  367.0 9.0 %all-to-all-done.13 = f32[16,32,256]{2,1,0:T(8,128)} async-done(((f32[16,32,256]{2,1,0:T(8,128)}), f32[16,32,256]{2,1,0:T(8,128)}, u32[]{:S(2)}, u32[]{:S(2)}) %all-to-all-start.13) | async-done | bytes 524320 | tf_op jit(solution)/shard_map/all_to_all | solution.py:45
  376.0 1.4 fusion.176
  378.6 3.5 all-to-all-start.14
  382.2 9.5 %collective-permute-start.16 = (f32[3,16,256]{2,1,0:T(8,128)S(1)}, f32[3,16,256]{2,1,0:T(8,128)S(1)}, u32[]{:S(2)}, u32[]{:S(2)}) collective-permute-start(f32[3,16,256]{2,1,0:T(8,128)S(1)} %get-tuple-element.47), channel_id=1, source_target_pairs={{0,12},{1,14},{2,6},{3,8},{4,0},{5,2},{6,10},{7,4},{8,13},{9,15},{... | collective-permute-start | bytes 147464 | tf_op jit(solution)/shard_map/ppermute | solution.py:217
  391.6 1.9 collective-permute-start.17
  393.8 9.2 %collective-permute-done.17 = f32[3,16,256]{2,1,0:T(8,128)S(1)} collective-permute-done((f32[3,16,256]{2,1,0:T(8,128)S(1)}, f32[3,16,256]{2,1,0:T(8,128)S(1)}, u32[]{:S(2)}, u32[]{:S(2)}) %collective-permute-start.17) | collective-permute-done | bytes 49184 | tf_op jit(solution)/shard_map/ppermute | solution.py:218
  403.0 1.9 collective-permute-start.14
  405.6 3.1 collective-permute-done.14
  (289 shorter events, 57.2 us)
Async XLA Ops:
  2.3 8.3 %copy-start.19 = (f32[1,3,1,1,1,1,256,256]{7,6,5,4,3,2,1,0:T(8,128)S(1)}, f32[1,3,1,1,1,1,256,256]{7,6,5,4,3,2,1,0:T(8,128)}, u32[]{:S(2)}) copy-start(f32[1,3,1,1,1,1,256,256]{7,6,5,4,3,2,1,0:T(8,128)} %param.18) | copy-start | bytes 2359300
  3.1 7.2 %copy-start.44 = (s32[1,4,3,1,1,1,1]{1,6,5,4,3,2,0:T(1,128)S(1)}, s32[1,4,3,1,1,1,1]{1,6,5,4,3,2,0:T(1,128)}, u32[]{:S(2)}) copy-start(s32[1,4,3,1,1,1,1]{1,6,5,4,3,2,0:T(1,128)} %param.22) | copy-start | bytes 148
  3.1 29.0 %all-to-all-start = ((f32[8,4,16,256]{3,2,1,0:T(8,128)}), f32[8,4,16,256]{3,2,1,0:T(8,128)S(1)}, u32[]{:S(2)}, u32[]{:S(2)}) async-start(f32[8,4,16,256]{3,2,1,0:T(8,128)} %broadcast_in_dim.113), calls=%async_computation | async-start | bytes 1048576 | tf_op jit(solution)/shard_map/all_to_all | solution.py:45
  10.7 6.1 %copy-start.42 = (f32[1,3,1,1,16,512]{5,4,3,2,1,0:T(8,128)S(1)}, f32[1,3,1,1,16,512]{5,4,3,2,1,0:T(8,128)}, u32[]{:S(2)}) copy-start(f32[1,3,1,1,16,512]{5,4,3,2,1,0:T(8,128)} %param.12) | copy-start | bytes 294916
  10.7 8.1 %copy-start.20 = (f32[1,3,1,1,1,1,256,256]{7,6,5,4,3,2,1,0:T(8,128)S(1)}, f32[1,3,1,1,1,1,256,256]{7,6,5,4,3,2,1,0:T(8,128)}, u32[]{:S(2)}) copy-start(f32[1,3,1,1,1,1,256,256]{7,6,5,4,3,2,1,0:T(8,128)} %param.19) | copy-start | bytes 2359300
  11.7 5.1 %copy-start.43 = (f32[1,1,16,512]{3,2,1,0:T(8,128)S(1)}, f32[1,1,16,512]{3,2,1,0:T(8,128)}, u32[]{:S(2)}) copy-start(f32[1,1,16,512]{3,2,1,0:T(8,128)} %param.13) | copy-start | bytes 98308
  11.7 96.1 %collective-permute-start.3 = (f32[1,256,256]{2,1,0:T(8,128)}, f32[1,256,256]{2,1,0:T(8,128)}, u32[]{:S(2)}, u32[]{:S(2)}) collective-permute-start(f32[1,256,256]{2,1,0:T(8,128)} %get-tuple-element.29), channel_id=1, source_target_pairs={{0,8},{8,0},{1,9},{9,1},{2,10},{10,2},{3,11},{11,3},{4,12},{12,4},... | collective-permute-start | bytes 786440 | tf_op jit(solution)/shard_map/ppermute | solution.py:110
  16.8 8.9 %collective-permute-start.2 = (f32[5,16,256]{2,1,0:T(8,128)S(1)}, f32[5,16,256]{2,1,0:T(8,128)S(1)}, u32[]{:S(2)}, u32[]{:S(2)}) collective-permute-start(f32[5,16,256]{2,1,0:T(8,128)S(1)} %pad_maximum_fusion.6), channel_id=1, source_target_pairs={{0,8},{8,0},{1,9},{9,1},{2,10},{10,2},{3,11},{11,3},{4,12},{12,4},... | collective-permute-start | bytes 245768 | tf_op jit(solution)/shard_map/ppermute | solution.py:100
  18.9 9.0 %copy-start.21 = (f32[1,3,1,1,1,1,256,256]{7,6,5,4,3,2,1,0:T(8,128)S(1)}, f32[1,3,1,1,1,1,256,256]{7,6,5,4,3,2,1,0:T(8,128)}, u32[]{:S(2)}) copy-start(f32[1,3,1,1,1,1,256,256]{7,6,5,4,3,2,1,0:T(8,128)} %param.21) | copy-start | bytes 2359300
  18.9 99.3 %collective-permute-start.6 = (f32[3,256,256]{2,1,0:T(8,128)S(1)}, f32[3,256,256]{2,1,0:T(8,128)}, u32[]{:S(2)}, u32[]{:S(2)}) collective-permute-start(f32[3,256,256]{2,1,0:T(8,128)S(1)} %bitcast_multiply_fusion.1), channel_id=1, source_target_pairs={{0,8},{8,0},{1,9},{9,1},{2,10},{10,2},{3,11},{11,3},{4,12},{12,4},... | collective-permute-start | bytes 2359304 | tf_op jit(solution)/shard_map/ppermute | solution.py:110
  23.8 92.6 %collective-permute-start.8 = (f32[2,256,256]{2,1,0:T(8,128)}, f32[2,256,256]{2,1,0:T(8,128)}, u32[]{:S(2)}, u32[]{:S(2)}) collective-permute-start(f32[2,256,256]{2,1,0:T(8,128)} %slice.327), channel_id=1, source_target_pairs={{0,8},{8,0},{1,9},{9,1},{2,10},{10,2},{3,11},{11,3},{4,12},{12,4},... | collective-permute-start | bytes 1572872 | tf_op jit(solution)/shard_map/ppermute | solution.py:110
  27.3 4.8 %collective-permute-start.4 = (f32[32,512]{1,0:T(8,128)S(1)}, f32[32,512]{1,0:T(8,128)S(1)}, u32[]{:S(2)}, u32[]{:S(2)}) collective-permute-start(f32[32,512]{1,0:T(8,128)S(1)} %pad_maximum_fusion.8), channel_id=1, source_target_pairs={{0,0},{1,16},{2,32},{3,48},{4,64},{5,80},{6,96},{7,112},{8,8},{9,2... | collective-permute-start | bytes 196616 | tf_op jit(solution)/shard_map/ppermute | solution.py:41
  28.1 231.0 %collective-permute-start.5 = (f32[3,256,256]{2,1,0:T(8,128)S(1)}, f32[3,256,256]{2,1,0:T(8,128)}, u32[]{:S(2)}, u32[]{:S(2)}) collective-permute-start(f32[3,256,256]{2,1,0:T(8,128)S(1)} %bitcast_multiply_fusion.2), channel_id=1, source_target_pairs={{0,8},{8,0},{1,9},{9,1},{2,10},{10,2},{3,11},{11,3},{4,12},{12,4},... | collective-permute-start | bytes 2359304 | tf_op jit(solution)/shard_map/ppermute | solution.py:110
  33.2 76.8 %all-to-all-start.1 = ((f32[16,32,512]{2,1,0:T(8,128)}), f32[16,32,512]{2,1,0:T(8,128)S(1)}, u32[]{:S(2)}, u32[]{:S(2)}) async-start(f32[16,32,512]{2,1,0:T(8,128)} %broadcast_in_dim.124), calls=%async_computation.1 | async-start | bytes 2097152 | tf_op jit(solution)/shard_map/all_to_all | solution.py:45
  55.9 115.1 %copy-start.46 = (s32[256]{0:T(256)}, s32[256]{0:T(256)S(1)}, u32[]{:S(2)}) copy-start(s32[256]{0:T(256)S(1)} %get-tuple-element.67) | copy-start | bytes 3076
  55.9 115.1 %copy-start.51 = (s32[256]{0:T(256)}, s32[256]{0:T(256)S(1)}, u32[]{:S(2)}) copy-start(s32[256]{0:T(256)S(1)} %get-tuple-element.68) | copy-start | bytes 3076
  56.4 114.5 %copy-start.56 = (s32[256]{0:T(256)}, s32[256]{0:T(256)S(1)}, u32[]{:S(2)}) copy-start(s32[256]{0:T(256)S(1)} %get-tuple-element.69) | copy-start | bytes 3076
  60.9 39.1 %collective-permute-start.1 = (f32[128,256]{0,1:T(8,128)}, f32[128,256]{0,1:T(8,128)}, u32[]{:S(2)}, u32[]{:S(2)}) collective-permute-start(f32[128,256]{0,1:T(8,128)} %copy.70), channel_id=1, source_target_pairs={{0,8},{8,0},{1,9},{9,1},{2,10},{10,2},{3,11},{11,3},{4,12},{12,4},... | collective-permute-start | bytes 393224 | tf_op jit(solution)/shard_map/ppermute | solution.py:93
  74.7 28.5 %copy-start.35 = (f32[128,256]{0,1:T(8,128)S(1)}, f32[128,256]{0,1:T(8,128)}, u32[]{:S(2)}) copy-start(f32[128,256]{0,1:T(8,128)} %copy.70) | copy-start | bytes 393220
  100.0 40.4 %collective-permute-start = (f32[3,128,256]{1,2,0:T(8,128)}, f32[3,128,256]{1,2,0:T(8,128)}, u32[]{:S(2)}, u32[]{:S(2)}) collective-permute-start(f32[3,128,256]{1,2,0:T(8,128)} %pad_maximum_fusion.1), channel_id=1, source_target_pairs={{0,8},{8,0},{1,9},{9,1},{2,10},{10,2},{3,11},{11,3},{4,12},{12,4},... | collective-permute-start | bytes 1179656 | tf_op jit(solution)/shard_map/ppermute | solution.py:94
  112.6 14.3 %all-to-all-start.2 = ((f32[8,32,256]{2,1,0:T(8,128)}), f32[8,32,256]{2,1,0:T(8,128)S(1)}, u32[]{:S(2)}, u32[]{:S(2)}) async-start(f32[8,32,256]{2,1,0:T(8,128)} %bitcast.34), calls=%async_computation.2 | async-start | bytes 524288 | tf_op jit(solution)/shard_map/all_to_all | solution.py:53
  126.9 16.9 %collective-permute-start.7 = (f32[32,256]{1,0:T(8,128)S(1)}, f32[32,256]{1,0:T(8,128)S(1)}, u32[]{:S(2)}, u32[]{:S(2)}) collective-permute-start(f32[32,256]{1,0:T(8,128)S(1)} %reduce_sum.63), channel_id=1, source_target_pairs={{0,96},{1,112},{2,48},{3,64},{4,0},{5,16},{6,80},{7,32},{8,104},{9... | collective-permute-start | bytes 98312 | tf_op jit(solution)/shard_map/ppermute | solution.py:41
  144.7 21.5 %all-to-all-start.3 = ((f32[16,32,256]{2,1,0:T(8,128)}), f32[16,32,256]{2,1,0:T(8,128)S(1)}, u32[]{:S(2)}, u32[]{:S(2)}) async-start(f32[16,32,256]{2,1,0:T(8,128)} %broadcast_in_dim.126), calls=%async_computation.3 | async-start | bytes 1048576 | tf_op jit(solution)/shard_map/all_to_all | solution.py:45
  167.3 3.6 copy-start.36
  167.3 3.6 copy-start.41
  167.3 3.6 copy-start.77
  167.3 13.9 %all-to-all-start.4 = ((f32[8,32,256]{2,1,0:T(8,128)}), f32[8,32,256]{2,1,0:T(8,128)S(1)}, u32[]{:S(2)}, u32[]{:S(2)}) async-start(f32[8,32,256]{2,1,0:T(8,128)} %bitcast.60), calls=%async_computation.4 | async-start | bytes 524288 | tf_op jit(solution)/shard_map/all_to_all | solution.py:53
  181.3 9.7 %collective-permute-start.9 = (f32[32,256]{1,0:T(8,128)S(1)}, f32[32,256]{1,0:T(8,128)S(1)}, u32[]{:S(2)}, u32[]{:S(2)}) collective-permute-start(f32[32,256]{1,0:T(8,128)S(1)} %reduce_sum.64), channel_id=1, source_target_pairs={{0,96},{1,112},{2,48},{3,64},{4,0},{5,16},{6,80},{7,32},{8,104},{9... | collective-permute-start | bytes 98312 | tf_op jit(solution)/shard_map/ppermute | solution.py:41
  191.9 10.1 %copy-start.12 = (f32[256,256]{1,0:T(8,128)S(1)}, f32[256,256]{1,0:T(8,128)}, u32[]{:S(2)}) copy-start(f32[256,256]{1,0:T(8,128)} %get-tuple-element.25) | copy-start | bytes 786436
  191.9 21.1 %all-to-all-start.5 = ((f32[16,32,256]{2,1,0:T(8,128)}), f32[16,32,256]{2,1,0:T(8,128)S(1)}, u32[]{:S(2)}, u32[]{:S(2)}) async-start(f32[16,32,256]{2,1,0:T(8,128)} %broadcast_in_dim.127), calls=%async_computation.5 | async-start | bytes 1048576 | tf_op jit(solution)/shard_map/all_to_all | solution.py:45
  219.9 12.9 %all-to-all-start.7 = ((f32[8,32,128]{2,1,0:T(8,128)}), f32[8,32,128]{2,1,0:T(8,128)S(1)}, u32[]{:S(2)}, u32[]{:S(2)}) async-start(f32[8,32,128]{2,1,0:T(8,128)} %bitcast.64), calls=%async_computation.7 | async-start | bytes 262144 | tf_op jit(solution)/shard_map/all_to_all | solution.py:53
  224.8 59.7 %collective-permute-start.11 = (f32[3,256,256]{2,1,0:T(8,128)S(1)}, f32[3,256,256]{2,1,0:T(8,128)}, u32[]{:S(2)}, u32[]{:S(2)}) collective-permute-start(f32[3,256,256]{2,1,0:T(8,128)S(1)} %bitcast_multiply_fusion), channel_id=1, source_target_pairs={{0,8},{8,0},{1,9},{9,1},{2,10},{10,2},{3,11},{11,3},{4,12},{12,4},... | collective-permute-start | bytes 2359304 | tf_op jit(solution)/shard_map/ppermute | solution.py:110
  232.9 13.4 %collective-permute-start.10 = (f32[32,128]{1,0:T(8,128)S(1)}, f32[32,128]{1,0:T(8,128)}, u32[]{:S(2)}, u32[]{:S(2)}) collective-permute-start(f32[32,128]{1,0:T(8,128)S(1)} %reduce_sum.66), channel_id=1, source_target_pairs={{0,96},{1,112},{2,48},{3,64},{4,0},{5,16},{6,80},{7,32},{8,104},{9... | collective-permute-start | bytes 49160 | tf_op jit(solution)/shard_map/ppermute | solution.py:41
  247.8 21.4 %all-to-all-start.8 = ((f32[16,32,128]{2,1,0:T(8,128)}), f32[16,32,128]{2,1,0:T(8,128)}, u32[]{:S(2)}, u32[]{:S(2)}) async-start(f32[16,32,128]{2,1,0:T(8,128)} %broadcast_in_dim.128), calls=%async_computation.8 | async-start | bytes 524288 | tf_op jit(solution)/shard_map/all_to_all | solution.py:45
  270.3 4.3 %copy-start.24 = (f32[256,512]{1,0:T(8,128)S(1)}, f32[256,512]{1,0:T(8,128)}, u32[]{:S(2)}) copy-start(f32[256,512]{1,0:T(8,128)} %fusion.50) | copy-start | bytes 1572868
  276.9 18.9 %all-to-all-start.10 = ((f32[8,32,256]{2,1,0:T(8,128)}), f32[8,32,256]{2,1,0:T(8,128)S(1)}, u32[]{:S(2)}, u32[]{:S(2)}) async-start(f32[8,32,256]{2,1,0:T(8,128)} %bitcast.75), calls=%async_computation.10 | async-start | bytes 524288 | tf_op jit(solution)/shard_map/all_to_all | solution.py:53
  284.5 14.9 %copy-start.31 = (f32[256,256]{1,0:T(8,128)S(1)}, f32[256,256]{1,0:T(8,128)}, u32[]{:S(2)}) copy-start(f32[256,256]{1,0:T(8,128)} %get-tuple-element.18) | copy-start | bytes 786436
  284.5 14.9 %copy-start.82 = (f32[256,256]{0,1:T(8,128)S(1)}, f32[256,256]{0,1:T(8,128)}, u32[]{:S(2)}) copy-start(f32[256,256]{0,1:T(8,128)} %get-tuple-element.62) | copy-start | bytes 786436
  286.5 12.9 %copy-start.30 = (f32[256,256]{1,0:T(8,128)S(1)}, f32[256,256]{1,0:T(8,128)}, u32[]{:S(2)}) copy-start(f32[256,256]{1,0:T(8,128)} %get-tuple-element.15) | copy-start | bytes 786436
  295.8 3.7 copy-start.54
  295.8 3.7 copy-start.59
  295.8 3.7 copy-start.66
  295.8 3.7 copy-start.80
  295.8 5.5 %copy-start.37 = (f32[32,256]{1,0:T(8,128)}, f32[32,256]{1,0:T(8,128)S(1)}, u32[]{:S(2)}) copy-start(f32[32,256]{1,0:T(8,128)S(1)} %reduce_sum.67) | copy-start | bytes 98308
  295.8 9.7 %collective-permute-start.12 = (f32[32,256]{1,0:T(8,128)S(1)}, f32[32,256]{1,0:T(8,128)S(1)}, u32[]{:S(2)}, u32[]{:S(2)}) collective-permute-start(f32[32,256]{1,0:T(8,128)S(1)} %reduce_sum.67), channel_id=1, source_target_pairs={{0,96},{1,112},{2,48},{3,64},{4,0},{5,16},{6,80},{7,32},{8,104},{9... | collective-permute-start | bytes 98312 | tf_op jit(solution)/shard_map/ppermute | solution.py:41
  306.4 7.9 %copy-start.32 = (f32[256,256]{1,0:T(8,128)S(1)}, f32[256,256]{1,0:T(8,128)}, u32[]{:S(2)}) copy-start(f32[256,256]{1,0:T(8,128)} %get-tuple-element.9) | copy-start | bytes 786436
  306.4 19.6 %all-to-all-start.11 = ((f32[16,32,256]{2,1,0:T(8,128)}), f32[16,32,256]{2,1,0:T(8,128)S(1)}, u32[]{:S(2)}, u32[]{:S(2)}) async-start(f32[16,32,256]{2,1,0:T(8,128)} %broadcast_in_dim.131), calls=%async_computation.11 | async-start | bytes 1048576 | tf_op jit(solution)/shard_map/all_to_all | solution.py:45
  327.1 14.8 %all-to-all-start.12 = ((f32[8,32,256]{2,1,0:T(8,128)}), f32[8,32,256]{2,1,0:T(8,128)S(1)}, u32[]{:S(2)}, u32[]{:S(2)}) async-start(f32[8,32,256]{2,1,0:T(8,128)} %bitcast.84), calls=%async_computation.12 | async-start | bytes 524288 | tf_op jit(solution)/shard_map/all_to_all | solution.py:53
  332.6 13.5 %copy-start.8 = (f32[256,256]{1,0:T(8,128)S(1)}, f32[256,256]{1,0:T(8,128)}, u32[]{:S(2)}) copy-start(f32[256,256]{1,0:T(8,128)} %get-tuple-element.17) | copy-start | bytes 786436
  341.9 4.7 %copy-start.39 = (f32[32,256]{1,0:T(8,128)}, f32[32,256]{1,0:T(8,128)S(1)}, u32[]{:S(2)}) copy-start(f32[32,256]{1,0:T(8,128)S(1)} %reduce_sum.68) | copy-start | bytes 98308
  342.0 9.8 %collective-permute-start.13 = (f32[32,256]{1,0:T(8,128)S(1)}, f32[32,256]{1,0:T(8,128)S(1)}, u32[]{:S(2)}, u32[]{:S(2)}) collective-permute-start(f32[32,256]{1,0:T(8,128)S(1)} %reduce_sum.68), channel_id=1, source_target_pairs={{0,96},{1,112},{2,48},{3,64},{4,0},{5,16},{6,80},{7,32},{8,104},{9... | collective-permute-start | bytes 98312 | tf_op jit(solution)/shard_map/ppermute | solution.py:41
  352.6 9.4 %copy-start.13 = (f32[256,256]{1,0:T(8,128)S(1)}, f32[256,256]{1,0:T(8,128)}, u32[]{:S(2)}) copy-start(f32[256,256]{1,0:T(8,128)} %get-tuple-element.10) | copy-start | bytes 786436
  352.6 9.4 %copy-start.15 = (f32[256,256]{1,0:T(8,128)S(1)}, f32[256,256]{1,0:T(8,128)}, u32[]{:S(2)}) copy-start(f32[256,256]{1,0:T(8,128)} %get-tuple-element.13) | copy-start | bytes 786436
  352.6 23.4 %all-to-all-start.13 = ((f32[16,32,256]{2,1,0:T(8,128)}), f32[16,32,256]{2,1,0:T(8,128)}, u32[]{:S(2)}, u32[]{:S(2)}) async-start(f32[16,32,256]{2,1,0:T(8,128)} %broadcast_in_dim.132), calls=%async_computation.13 | async-start | bytes 1048576 | tf_op jit(solution)/shard_map/all_to_all | solution.py:45
  362.0 2.4 copy-start.10
  362.5 3.2 collective-permute-start.15
  378.6 3.6 copy-start.38
  378.6 3.6 copy-start.40
  378.6 24.4 %all-to-all-start.14 = ((f32[8,32,256]{2,1,0:T(8,128)}), f32[8,32,256]{2,1,0:T(8,128)S(1)}, u32[]{:S(2)}, u32[]{:S(2)}) async-start(f32[8,32,256]{2,1,0:T(8,128)} %bitcast.86), calls=%async_computation.14 | async-start | bytes 524288 | tf_op jit(solution)/shard_map/all_to_all | solution.py:53
  382.2 11.6 %collective-permute-start.16 = (f32[3,16,256]{2,1,0:T(8,128)S(1)}, f32[3,16,256]{2,1,0:T(8,128)S(1)}, u32[]{:S(2)}, u32[]{:S(2)}) collective-permute-start(f32[3,16,256]{2,1,0:T(8,128)S(1)} %get-tuple-element.47), channel_id=1, source_target_pairs={{0,12},{1,14},{2,6},{3,8},{4,0},{5,2},{6,10},{7,4},{8,13},{9,15},{... | collective-permute-start | bytes 147464 | tf_op jit(solution)/shard_map/ppermute | solution.py:217
  391.6 11.3 %collective-permute-start.17 = (f32[3,16,256]{2,1,0:T(8,128)S(1)}, f32[3,16,256]{2,1,0:T(8,128)S(1)}, u32[]{:S(2)}, u32[]{:S(2)}) collective-permute-start(f32[3,16,256]{2,1,0:T(8,128)S(1)} %get-tuple-element.48), channel_id=1, source_target_pairs={{0,13},{1,15},{2,7},{3,9},{4,1},{5,3},{6,11},{7,5},{8,12},{9,14},{... | collective-permute-start | bytes 147464 | tf_op jit(solution)/shard_map/ppermute | solution.py:218
  403.0 2.6 copy-start.28
  403.0 5.6 %collective-permute-start.14 = (f32[16,256]{1,0:T(8,128)S(1)}, f32[16,256]{1,0:T(8,128)S(1)}, u32[]{:S(2)}, u32[]{:S(2)}) collective-permute-start(f32[16,256]{1,0:T(8,128)S(1)} %get-tuple-element.52), channel_id=1, source_target_pairs={{0,8},{8,0},{1,9},{9,1},{2,10},{10,2},{3,11},{11,3},{4,12},{12,4},... | collective-permute-start | bytes 49160 | tf_op jit(solution)/shard_map/ppermute | solution.py:222
  405.6 3.1 slice-start
  (55 other events, 59.4 us)
